TPU v7x, 256 devices: a whole 4x4x8 slice. The times are simulated.
256 devices in a mesh: sec: 8 (over y, core), dom: 32 (over x, z).
Axes of the slice: x: 4, y: 4, z: 8, core: 2. Of those that a mesh axis runs over, the one named last changes fastest.
Arguments:
- flow_state: bfloat16 [270, 262144], P(None, ('sec', 'dom')), may hold values from -6 to 6
- base_geometry: float32 [4, 262144], P(None, ('sec', 'dom')), may hold values from 0.5 to 2
- anchor_weight: float32 [262144], P(('sec', 'dom')), may hold values from 0 to 1.5
- wall_anchor: int32 [262144], P(('sec', 'dom')), may hold values from 0 to 262143
- face_nbr: int32 [6, 262144], P(None, ('sec', 'dom')), may hold values from 0 to 1151, as said below
- volume_ops: bfloat16 [4, 270, 270], replicated, may hold values from -0.375 to 0.375
- lift_ops: bfloat16 [6, 270, 90], replicated, may hold values from -0.625 to 0.625
- face_jac: bfloat16 [6, 2, 5, 5], replicated, may hold values from -2.5 to 2.5
- wall_load: float32 [3, 2048, 128], P(None, ('sec', 'dom')), may hold values from -6 to 6
- wall_stiff: float32 [3, 2048, 128], P(None, ('sec', 'dom')), may hold values from 0.01 to 0.3
Outputs:
- flow_residual: bfloat16 [270, 262144], P(None, ('sec', 'dom'))
- wall_disp: float32 [3, 2048, 128], P(None, ('sec', 'dom'))
Inputs may be any that keep to these rules, and one draw needn't show every extreme that they name: `face_nbr`: for faces 0 to 3 a value v >= 1024 names element v - 1024 (below 128) of the device one step lower (faces 0 and 2) or higher (faces 1 and 3), cyclically, along dom (faces 0 and 1) or sec (faces 2 and 3); a smaller value names an element of the element's own device. Faces 4 and 5 always name an element of the own device.
All inputs are finite; a program needn't handle non-finite values.
Results may differ from a plain program's by a relative error of at most 0.0046.
Values may be sent and summed in bfloat16 or wider, within the bound.
A program may use at most 320 MiB of HBM per device.

v0:
```python
import jax
import jax.numpy as jnp
from jax import lax
from jax.sharding import PartitionSpec as P

NV = 5
ITERS = 8


def padded_2(x, sides, width):
    for axis, dim in sides:
        peers, length = (lax.axis_size(axis), x.shape[dim])
        up = [(i, (i + 1) % peers) for i in range(peers - 1)]
        down = [(j, i) for i, j in up]
        last = lax.slice_in_dim(x, length - width, length, axis=dim)
        leading = lax.slice_in_dim(x, 0, width, axis=dim)
        before = lax.ppermute(last, axis, up)
        after = lax.ppermute(leading, axis, down)
        x = jnp.concatenate([before, x, after], axis=dim)
    return x


def shifted(x, axis, by):
    peers = lax.axis_size(axis)
    return lax.ppermute(x, axis, [(i, (i + by) % peers) for i in range(peers)])


def wall_operator(field, stiffness):
    padded = padded_2(field, ((("sec", "dom"), 1),), 1)
    padded = jnp.pad(padded, ((0, 0), (0, 0), (1, 1)))
    beside = padded[:, 2:, 1:-1] + padded[:, :-2, 1:-1] + padded[:, 1:-1, 2:] + padded[:, 1:-1, :-2]
    return (4.0 + stiffness) * field - beside


def squares(resid):
    return lax.psum(jnp.sum(resid * resid), ("sec", "dom"))


def face_trace(values, face):
    shaped = values.reshape(NV, 2, 3, 3, 3, values.shape[1])
    picked = lax.index_in_dim(shaped, 0 if face % 2 == 0 else 2, 2 + face // 2, keepdims=False)
    return picked.reshape(NV * 18, values.shape[1])


def shift_dom(values, offset):
    return shifted(values, "dom", offset)


def shift_sec(values, offset):
    return shifted(values, "sec", offset)


def split_solve(wall_load, wall_stiff):

    def iterate(position, carry):
        wall_disp, resid, search, norm_now = carry
        image = wall_operator(search, wall_stiff)
        step_size = norm_now / lax.psum(jnp.sum(search * image), ("sec", "dom"))
        wall_disp = wall_disp + step_size * search
        resid = resid - step_size * image
        norm_next = squares(resid)
        search = resid + norm_next / norm_now * search
        return (wall_disp, resid, search, norm_next)

    start_carry = (jnp.zeros_like(wall_load), wall_load, wall_load, squares(wall_load))
    wall_disp = lax.fori_loop(0, ITERS, iterate, start_carry)[0]
    return wall_disp


def on_device(
    flow_state,
    base_geometry,
    anchor_weight,
    wall_anchor,
    face_nbr,
    volume_ops,
    lift_ops,
    face_jac,
    wall_load,
    wall_stiff,
):
    wall_disp = split_solve(wall_load, wall_stiff)
    gathered = lax.all_gather(wall_disp, ("sec", "dom"), axis=1, tiled=True)
    flattened = gathered.reshape(3, gathered.shape[1] * gathered.shape[2])
    disp_at = jnp.take(flattened, wall_anchor, axis=1)
    geometry = jnp.concatenate(
        [base_geometry[:3] * jnp.exp(anchor_weight[None, :] * disp_at), base_geometry[3:]], axis=0
    )
    head_count = flow_state.shape[1] // 8
    head_block = flow_state[:, :head_count]
    remotes = [
        shift_dom(face_trace(head_block, 1), 1),
        shift_dom(face_trace(head_block, 0), -1),
        shift_sec(face_trace(head_block, 3), 1),
        shift_sec(face_trace(head_block, 2), -1),
    ]
    summed = jnp.zeros(flow_state.shape, jnp.float32)
    for direction in range(4):
        summed = summed + geometry[direction][None, :] * jnp.dot(
            volume_ops[direction], flow_state, preferred_element_type=jnp.float32
        )
    identity = jnp.eye(18, dtype=jnp.bfloat16)
    for face in range(6):
        own_trace = face_trace(flow_state, face)
        opposite = face_trace(flow_state, face ^ 1)
        if face < 4:
            candidates = jnp.concatenate([opposite, remotes[face]], axis=1)
        else:
            candidates = opposite
        neighbour_trace = jnp.take(candidates, face_nbr[face], axis=1)
        own_jac = jnp.kron(face_jac[face, 0], identity)
        other_jac = jnp.kron(face_jac[face, 1], identity)
        face_flux = geometry[face // 2][None, :] * (
            jnp.dot(own_jac, own_trace, preferred_element_type=jnp.float32)
            + jnp.dot(other_jac, neighbour_trace, preferred_element_type=jnp.float32)
        )
        face_flux = face_flux.astype(jnp.bfloat16)
        summed = summed + jnp.dot(lift_ops[face], face_flux, preferred_element_type=jnp.float32)
    return (summed.astype(jnp.bfloat16), wall_disp)


def solution(mesh):
    return jax.shard_map(
        on_device,
        mesh=mesh,
        in_specs=(
            P(None, ("sec", "dom")),
            P(None, ("sec", "dom")),
            P(("sec", "dom")),
            P(("sec", "dom")),
            P(None, ("sec", "dom")),
            P(),
            P(),
            P(),
            P(None, ("sec", "dom"), None),
            P(None, ("sec", "dom"), None),
        ),
        out_specs=(P(None, ("sec", "dom")), P(None, ("sec", "dom"), None)),
        check_vma=False,
    )
```

profile of v0, /device:TPU:1, one launch (start us, length us, event | category | flops | bytes accessed | tf_op | source)
XLA Modules:
  0.0 1593.5 jit_solution(9426961634157462458)
XLA Ops:
  12.9 79.1 %psum.27 = f32[]{:T(128)} all-reduce(f32[]{:T(128)} %multiply_reduce_fusion.2), channel_id=1, replica_groups=mesh['sec'=8,'dom'=32] {'sec','dom'}, use_global_device_ids=true, to_apply=%region_1.0 | all-reduce | flops 1 | bytes 8 | tf_op jit(solution)/shard_map/psum | solution.py:36
  92.1 1298.5 %while.19 = (s32[]{:T(128)}, f32[3,8,128]{2,1,0:T(8,128)S(1)}, f32[3,8,128]{2,1,0:T(8,128)S(1)}, f32[3,8,128]{2,1,0:T(8,128)S(1)}, f32[]{:T(128)}, /*index=5*/f32[3,8,128]{2,1,0:T(8,128)}, s32[]{:T(128)}, s32[]{:T(128)}) while((s32[]{:T(128)}, f32[3,8,128]{2,1,0:T(8,128)S(1)}, f32[3,8,128]{2,1,0:T(8,128)S(1)}, ...), condition=%wide.region_7.8_spmd.clone, body=%wide.region_2.7_spmd.clone.sunk | while | flops 89573 | bytes 212451 | solution.py:66
  99.1 5.6 collective-permute-done.1
  106.2 72.5 %psum.32 = f32[]{:T(128)} all-reduce(f32[]{:T(128)} %get-tuple-element.218), channel_id=1, replica_groups=mesh['sec'=8,'dom'=32] {'sec','dom'}, use_global_device_ids=true, to_apply=%region_4.4 | all-reduce | flops 1 | bytes 8 | tf_op jit(solution)/shard_map/while/body/eval_jaxpr/psum | solution.py:58
  180.0 73.4 %psum.33 = f32[]{:T(128)} all-reduce(f32[]{:T(128)} %get-tuple-element.220), channel_id=1, replica_groups=mesh['sec'=8,'dom'=32] {'sec','dom'}, use_global_device_ids=true, to_apply=%region_6.6 | all-reduce | flops 1 | bytes 8 | tf_op jit(solution)/shard_map/while/body/eval_jaxpr/psum | solution.py:36
  261.5 5.6 collective-permute-done.1
  268.6 72.5 %psum.32 = f32[]{:T(128)} all-reduce(f32[]{:T(128)} %get-tuple-element.218), channel_id=1, replica_groups=mesh['sec'=8,'dom'=32] {'sec','dom'}, use_global_device_ids=true, to_apply=%region_4.4 | all-reduce | flops 1 | bytes 8 | tf_op jit(solution)/shard_map/while/body/eval_jaxpr/psum | solution.py:58
  342.3 73.4 %psum.33 = f32[]{:T(128)} all-reduce(f32[]{:T(128)} %get-tuple-element.220), channel_id=1, replica_groups=mesh['sec'=8,'dom'=32] {'sec','dom'}, use_global_device_ids=true, to_apply=%region_6.6 | all-reduce | flops 1 | bytes 8 | tf_op jit(solution)/shard_map/while/body/eval_jaxpr/psum | solution.py:36
  423.9 5.6 collective-permute-done.1
  431.0 72.4 %psum.32 = f32[]{:T(128)} all-reduce(f32[]{:T(128)} %get-tuple-element.218), channel_id=1, replica_groups=mesh['sec'=8,'dom'=32] {'sec','dom'}, use_global_device_ids=true, to_apply=%region_4.4 | all-reduce | flops 1 | bytes 8 | tf_op jit(solution)/shard_map/while/body/eval_jaxpr/psum | solution.py:58
  504.6 73.4 %psum.33 = f32[]{:T(128)} all-reduce(f32[]{:T(128)} %get-tuple-element.220), channel_id=1, replica_groups=mesh['sec'=8,'dom'=32] {'sec','dom'}, use_global_device_ids=true, to_apply=%region_6.6 | all-reduce | flops 1 | bytes 8 | tf_op jit(solution)/shard_map/while/body/eval_jaxpr/psum | solution.py:36
  586.2 5.6 collective-permute-done.1
  593.4 72.3 %psum.32 = f32[]{:T(128)} all-reduce(f32[]{:T(128)} %get-tuple-element.218), channel_id=1, replica_groups=mesh['sec'=8,'dom'=32] {'sec','dom'}, use_global_device_ids=true, to_apply=%region_4.4 | all-reduce | flops 1 | bytes 8 | tf_op jit(solution)/shard_map/while/body/eval_jaxpr/psum | solution.py:58
  666.9 73.4 %psum.33 = f32[]{:T(128)} all-reduce(f32[]{:T(128)} %get-tuple-element.220), channel_id=1, replica_groups=mesh['sec'=8,'dom'=32] {'sec','dom'}, use_global_device_ids=true, to_apply=%region_6.6 | all-reduce | flops 1 | bytes 8 | tf_op jit(solution)/shard_map/while/body/eval_jaxpr/psum | solution.py:36
  741.1 4.9 collective-permute-start
  748.6 5.6 collective-permute-done.1
  755.7 72.3 %psum.32 = f32[]{:T(128)} all-reduce(f32[]{:T(128)} %get-tuple-element.218), channel_id=1, replica_groups=mesh['sec'=8,'dom'=32] {'sec','dom'}, use_global_device_ids=true, to_apply=%region_4.4 | all-reduce | flops 1 | bytes 8 | tf_op jit(solution)/shard_map/while/body/eval_jaxpr/psum | solution.py:58
  829.4 73.4 %psum.33 = f32[]{:T(128)} all-reduce(f32[]{:T(128)} %get-tuple-element.220), channel_id=1, replica_groups=mesh['sec'=8,'dom'=32] {'sec','dom'}, use_global_device_ids=true, to_apply=%region_6.6 | all-reduce | flops 1 | bytes 8 | tf_op jit(solution)/shard_map/while/body/eval_jaxpr/psum | solution.py:36
  903.5 4.9 collective-permute-start
  911.0 5.6 collective-permute-done.1
  918.1 72.2 %psum.32 = f32[]{:T(128)} all-reduce(f32[]{:T(128)} %get-tuple-element.218), channel_id=1, replica_groups=mesh['sec'=8,'dom'=32] {'sec','dom'}, use_global_device_ids=true, to_apply=%region_4.4 | all-reduce | flops 1 | bytes 8 | tf_op jit(solution)/shard_map/while/body/eval_jaxpr/psum | solution.py:58
  991.7 73.4 %psum.33 = f32[]{:T(128)} all-reduce(f32[]{:T(128)} %get-tuple-element.220), channel_id=1, replica_groups=mesh['sec'=8,'dom'=32] {'sec','dom'}, use_global_device_ids=true, to_apply=%region_6.6 | all-reduce | flops 1 | bytes 8 | tf_op jit(solution)/shard_map/while/body/eval_jaxpr/psum | solution.py:36
  1065.8 5.0 collective-permute-start
  1073.4 5.6 collective-permute-done.1
  1080.5 72.3 %psum.32 = f32[]{:T(128)} all-reduce(f32[]{:T(128)} %get-tuple-element.218), channel_id=1, replica_groups=mesh['sec'=8,'dom'=32] {'sec','dom'}, use_global_device_ids=true, to_apply=%region_4.4 | all-reduce | flops 1 | bytes 8 | tf_op jit(solution)/shard_map/while/body/eval_jaxpr/psum | solution.py:58
  1154.1 73.4 %psum.33 = f32[]{:T(128)} all-reduce(f32[]{:T(128)} %get-tuple-element.220), channel_id=1, replica_groups=mesh['sec'=8,'dom'=32] {'sec','dom'}, use_global_device_ids=true, to_apply=%region_6.6 | all-reduce | flops 1 | bytes 8 | tf_op jit(solution)/shard_map/while/body/eval_jaxpr/psum | solution.py:36
  1235.8 5.6 collective-permute-done.1
  1242.9 72.2 %psum.32 = f32[]{:T(128)} all-reduce(f32[]{:T(128)} %get-tuple-element.218), channel_id=1, replica_groups=mesh['sec'=8,'dom'=32] {'sec','dom'}, use_global_device_ids=true, to_apply=%region_4.4 | all-reduce | flops 1 | bytes 8 | tf_op jit(solution)/shard_map/while/body/eval_jaxpr/psum | solution.py:58
  1316.4 73.4 %psum.33 = f32[]{:T(128)} all-reduce(f32[]{:T(128)} %get-tuple-element.220), channel_id=1, replica_groups=mesh['sec'=8,'dom'=32] {'sec','dom'}, use_global_device_ids=true, to_apply=%region_6.6 | all-reduce | flops 1 | bytes 8 | tf_op jit(solution)/shard_map/while/body/eval_jaxpr/psum | solution.py:36
  1453.0 40.2 %all-gather.2.cloned.1.call-done = f32[3,2048,128]{2,1,0:T(8,128)} async-done(((f32[3,8,128]{2,1,0:T(8,128)}), f32[3,2048,128]{2,1,0:T(8,128)}) %all-gather.2.cloned.1.call-update) | async-done | bytes 3145744 | tf_op jit(solution)/shard_map/all_gather | solution.py:83
  1493.2 60.6 %copy.36 = f32[3,2048,128]{0,2,1:T(8,128)} copy(f32[3,2048,128]{2,1,0:T(8,128)} %all-gather.2.cloned.1.call-done) | data formatting | bytes 6291456 | tf_op jit(solution)/shard_map/all_gather | solution.py:83
  1553.8 10.5 gather_fusion
  (218 shorter events, 145.9 us)
Async XLA Ops:
  7.2 1486.0 %all-gather.2.cloned.1.call-start = ((), (), s32[]{:S(2)}) async-start(), calls=%async_computation | async-start | bytes 3158016 | tf_op jit(solution)/shard_map/all_gather | solution.py:83
  8.8 1388.1 %copy-start = (bf16[270,1024]{1,0:T(8,128)(2,1)S(1)}, bf16[270,1024]{1,0:T(8,128)(2,1)}, u32[]{:S(2)}) copy-start(bf16[270,1024]{1,0:T(8,128)(2,1)} %param.16) | copy-start | bytes 1658884
  9.6 1423.9 %collective-permute-start.4 = (bf16[90,128]{0,1:T(8,128)(2,1)}, bf16[90,128]{0,1:T(8,128)(2,1)}, u32[]{:S(2)}, u32[]{:S(2)}) collective-permute-start(bf16[90,128]{0,1:T(8,128)(2,1)} %copy.52), channel_id=1, source_target_pairs={{0,32},{32,64},{64,96},{96,128},{128,160},{160,192},{192,224},{224... | collective-permute-start | bytes 69128 | tf_op jit(solution)/shard_map/ppermute | solution.py:25
  92.1 7.0 collective-permute-start
  96.5 8.2 collective-permute-start.1
  254.2 7.3 collective-permute-start
  258.9 8.2 collective-permute-start.1
  416.5 7.4 collective-permute-start
  421.3 8.2 collective-permute-start.1
  578.8 7.4 collective-permute-start
  583.6 8.2 collective-permute-start.1
  741.1 7.5 collective-permute-start
  746.0 8.2 collective-permute-start.1
  903.5 7.5 collective-permute-start
  908.4 8.2 collective-permute-start.1
  1065.8 7.6 collective-permute-start
  1070.8 8.2 collective-permute-start.1
  1228.3 7.5 collective-permute-start
  1233.2 8.2 collective-permute-start.1
  1392.0 42.4 %collective-permute-start.3 = (bf16[90,128]{0,1:T(8,128)(2,1)}, bf16[90,128]{0,1:T(8,128)(2,1)}, u32[]{:S(2)}, u32[]{:S(2)}) collective-permute-start(bf16[90,128]{0,1:T(8,128)(2,1)} %copy.48), channel_id=1, source_target_pairs={{0,31},{1,0},{2,1},{3,2},{4,3},{5,4},{6,5},{7,6},{8,7},{9,8},{10,9... | collective-permute-start | bytes 69128 | tf_op jit(solution)/shard_map/ppermute | solution.py:25
  1395.3 39.9 %collective-permute-start.2 = (bf16[90,128]{0,1:T(8,128)(2,1)}, bf16[90,128]{0,1:T(8,128)(2,1)}, u32[]{:S(2)}, u32[]{:S(2)}) collective-permute-start(bf16[90,128]{0,1:T(8,128)(2,1)} %copy.44), channel_id=1, source_target_pairs={{0,1},{1,2},{2,3},{3,4},{4,5},{5,6},{6,7},{7,8},{8,9},{9,10},{10,1... | collective-permute-start | bytes 69128 | tf_op jit(solution)/shard_map/ppermute | solution.py:25
  1396.0 51.8 %collective-permute-start.5 = (bf16[90,128]{0,1:T(8,128)(2,1)}, bf16[90,128]{0,1:T(8,128)(2,1)}, u32[]{:S(2)}, u32[]{:S(2)}) collective-permute-start(bf16[90,128]{0,1:T(8,128)(2,1)} %copy.56), channel_id=1, source_target_pairs={{0,224},{32,0},{64,32},{96,64},{128,96},{160,128},{192,160},{224,1... | collective-permute-start | bytes 69128 | tf_op jit(solution)/shard_map/ppermute | solution.py:25
  1411.6 3.0 copy-start.1
  1418.4 6.1 copy-start.9
  1453.0 100.8 %copy-start.15 = (s32[1024]{0:T(1024)S(1)}, s32[1024]{0:T(1024)}, u32[]{:S(2)}) copy-start(s32[1024]{0:T(1024)} %fusion.92) | copy-start | bytes 12292
  1453.0 111.3 %copy-start.17 = (f32[1024]{0:T(1024)S(1)}, f32[1024]{0:T(1024)}, u32[]{:S(2)}) copy-start(f32[1024]{0:T(1024)} %param.18) | copy-start | bytes 12292
  1453.0 111.4 %copy-start.19 = (pred[1024]{0:T(1024)(128)(4,1)S(1)}, pred[1024]{0:T(1024)(128)(4,1)}, u32[]{:S(2)}) copy-start(pred[1024]{0:T(1024)(128)(4,1)} %compare_and_fusion.6) | copy-start | bytes 3076
  1574.9 2.7 copy-start.7
  1574.9 2.7 copy-start.18
  1580.0 3.6 copy-start.3
  1580.0 3.6 copy-start.8
  1580.1 3.6 copy-start.20
  (10 other events, 12.3 us)
Sparse Core Ops, SparseCore 0:
  1391.3 101.8 all-gather.1
where the time goes:
time: 1600 us; the launch traced here: 1590 us
  blocking collectives  1250 us (78%)
  local copies, waits for them, and re-layouts  120 us (8%)
  waiting for transfers between devices  85.3 us (5%)
  starting transfers between devices  60 us (4%)
  other arithmetic  26.9 us (2%)
  matrix products  25 us (2%)
  loops' own time  16.5 us (1%)
    psum x9, blocking collectives, squares(): return lax.psum(jnp.sum(resid * resid), ('sec', 'dom'))  667 us
    psum x8, blocking collectives, iterate(): step_size = norm_now / lax.psum(jnp.sum(search * image), ('sec', 'dom'))  579 us
    all_gather x1, local copies, waits for them, and re-layouts, on_device(): gathered = lax.all_gather(wall_disp, ('sec', 'dom'), axis=1, tiled=True)  60.6 us
    ppermute x8, waiting for transfers between devices, padded_2(): before = lax.ppermute(last, axis, up)  45 us
    all_gather x1, waiting for transfers between devices, on_device(): gathered = lax.all_gather(wall_disp, ('sec', 'dom'), axis=1, tiled=True)  40.2 us
    ppermute x8, starting transfers between devices, padded_2(): after = lax.ppermute(leading, axis, down)  38.4 us
  transfers between devices with their start and end apart: 21, of which 9 were waited for; matrix products, arithmetic and copies ran while one was open for 5% of the time, Pallas kernels for 0%

commit v1 on v0

v1 whole, which is shorter than its diff:
```python
import functools

import jax
import jax.numpy as jnp
import numpy as np
from jax import lax
from jax.experimental import pallas as pl
from jax.experimental.pallas import tpu as pltpu
from jax.sharding import PartitionSpec as P

MESH = pl.DeviceIdType.MESH
ITERS = 8
NQ = 270
NF = 90
NE = 1024
HB = 128
NY, NC, NX, NZ = 4, 2, 4, 8
SIZE = {"y": NY, "x": NX, "z": NZ}
ORDERS = (("z", "x", "y"), ("x", "y", "z"), ("y", "z", "x"))
STEPS = sum(SIZE.values()) // 2
F32 = jnp.float32
BF16 = jnp.bfloat16


def selection():
    index = np.arange(NQ).reshape(5, 2, 3, 3, 3)
    rows = np.zeros((6, 128, NQ), np.float32)
    for face in range(6):
        picked = np.take(index, 0 if face % 2 == 0 else 2, axis=2 + face // 2).reshape(-1)
        rows[face, np.arange(NF), picked] = 1.0
    return rows


def expansion():
    spread = np.zeros((128, 5), np.float32)
    spread[np.arange(NF), np.arange(NF) // 18] = 1.0
    same = np.zeros((128, 128), np.float32)
    inside = np.arange(NF)
    same[:NF, :NF] = inside[:, None] % 18 == inside[None, :] % 18
    return spread, same


def coordinates():
    sec, dom = lax.axis_index("sec"), lax.axis_index("dom")
    return {"y": sec // NC, "core": sec % NC, "x": dom // NZ, "z": dom % NZ}


def device(place):
    return (place["y"] * NC + place["core"], place["x"] * NZ + place["z"])


def moved(place, axis, by):
    size = SIZE[axis]
    return dict(place, **{axis: (place[axis] + by + size) % size})


class Gather:
    def __init__(self, color, here, wall, send, recv, pass_send, pass_recv):
        self.color, self.here, self.wall = color, here, wall
        self.send, self.recv = send, recv
        self.pass_send, self.pass_recv = pass_send, pass_recv
        self.plan = []
        for stage, axis in enumerate(ORDERS[color]):
            for step in range(SIZE[axis] // 2):
                self.plan.append((stage, axis, step))
        self.passed = []

    def block(self, stage, axis, at, half):
        order = ORDERS[self.color]
        index = {}
        for name in "yxz":
            if name in order[:stage]:
                index[name] = slice(None)
            elif name == axis:
                index[name] = at
            else:
                index[name] = self.here[name]
        which = slice(None) if half is None else half
        return self.wall.at[self.color, which, index["y"], self.here["core"], index["x"], index["z"]]

    def copies(self, number):
        stage, axis, step = self.plan[number]
        size = SIZE[axis]
        made = []
        for way, sign in enumerate((1, -1)):
            half = None if step < size // 2 - 1 else way
            at = (self.here[axis] - sign * step + size) % size
            source = self.block(stage, axis, at, half)
            slot = (self.color * STEPS + number) * 2 + way
            made.append(
                pltpu.make_async_remote_copy(
                    src_ref=source,
                    dst_ref=source,
                    send_sem=self.send.at[slot],
                    recv_sem=self.recv.at[slot],
                    device_id=device(moved(self.here, axis, sign)),
                    device_id_type=MESH,
                )
            )
        return made

    def hand_over(self, at):
        axis = ORDERS[self.color][2]
        slot = self.color * NZ + len(self.passed)
        source = self.block(2, axis, at, None)
        copy = pltpu.make_async_remote_copy(
            src_ref=source,
            dst_ref=source,
            send_sem=self.pass_send.at[slot],
            recv_sem=self.pass_recv.at[slot],
            device_id=device(dict(self.here, core=1 - self.here["core"])),
            device_id_type=MESH,
        )
        copy.start()
        self.passed.append(copy)

    def advance(self, number):
        if number > 0:
            stage, axis, step = self.plan[number - 1]
            for copy in self.copies(number - 1):
                copy.wait_recv()
            if stage == 2:
                size = SIZE[axis]
                self.hand_over((self.here[axis] - step - 1 + size) % size)
                if step < size // 2 - 1:
                    self.hand_over((self.here[axis] + step + 1) % size)
        if number < STEPS:
            stage, axis, step = self.plan[number]
            for copy in self.copies(number):
                copy.start()
            if stage == 2 and step == 0:
                self.hand_over(self.here[axis])

    def finish(self):
        for number in range(STEPS):
            for copy in self.copies(number):
                copy.wait_send()
        for copy in self.passed:
            copy.wait()


def exchange_kernel(load, stiff, flow, wall, heads, send, recv, pass_send, pass_recv, head_send, head_recv, own_sem):
    here = coordinates()
    sec, dom = lax.axis_index("sec"), lax.axis_index("dom")
    n_sec, n_dom = NY * NC, NX * NZ
    sides = [
        (sec, (dom + 1) % n_dom),
        (sec, (dom + n_dom - 1) % n_dom),
        ((sec + 1) % n_sec, dom),
        ((sec + n_sec - 1) % n_sec, dom),
    ]
    peers = list(sides)
    for axis in "yxz":
        peers.append(device(moved(here, axis, 1)))
        peers.append(device(moved(here, axis, -1)))
    peers.append(device(dict(here, core=1 - here["core"])))
    own = wall.at[:, :, here["y"], here["core"], here["x"], here["z"]]
    mine = [
        pltpu.make_async_copy(load, own.at[:, 0], own_sem.at[0]),
        pltpu.make_async_copy(stiff, own.at[:, 1], own_sem.at[1]),
    ]
    for copy in mine:
        copy.start()
    barrier = pltpu.get_barrier_semaphore()
    for peer in peers:
        pl.semaphore_signal(barrier, inc=1, device_id=peer, device_id_type=MESH)
    pl.semaphore_wait(barrier, len(peers))
    for copy in mine:
        copy.wait()
    gathers = [Gather(color, here, wall, send, recv, pass_send, pass_recv) for color in range(3)]
    head_copies = []
    for number in range(STEPS + 1):
        for gather in gathers:
            gather.advance(number)
        if number == 0:
            for face, peer in enumerate(sides):
                copy = pltpu.make_async_remote_copy(
                    src_ref=flow.at[:, pl.ds(0, HB)],
                    dst_ref=heads.at[face],
                    send_sem=head_send.at[face],
                    recv_sem=head_recv.at[face],
                    device_id=peer,
                    device_id_type=MESH,
                )
                copy.start()
                head_copies.append(copy)
    for copy in head_copies:
        copy.wait()
    for gather in gathers:
        gather.finish()


def exchange(wall_load, wall_stiff, flow_state):
    vmem = pl.BlockSpec(memory_space=pltpu.VMEM)
    slots = 3 * STEPS * 2
    return pl.pallas_call(
        exchange_kernel,
        out_shape=(
            jax.ShapeDtypeStruct((3, 2, NY, NC, NX, NZ, 8, 128), F32),
            jax.ShapeDtypeStruct((4, NQ, HB), BF16),
        ),
        in_specs=[vmem] * 3,
        out_specs=(vmem, vmem),
        scratch_shapes=[
            pltpu.SemaphoreType.DMA((slots,)),
            pltpu.SemaphoreType.DMA((slots,)),
            pltpu.SemaphoreType.DMA((3 * NZ,)),
            pltpu.SemaphoreType.DMA((3 * NZ,)),
            pltpu.SemaphoreType.DMA((4,)),
            pltpu.SemaphoreType.DMA((4,)),
            pltpu.SemaphoreType.DMA((2,)),
        ],
        compiler_params=pltpu.CompilerParams(
            collective_id=0, has_side_effects=True, vmem_limit_bytes=16 << 20
        ),
        name="exchange",
    )(wall_load, wall_stiff, flow_state)


def dot(a, b):
    return jnp.dot(a, b, preferred_element_type=F32)


def residual_parts(flow, heads, nbr, vol, lift, jac, sel, spread, same, products, jumps, lifts, cand, pair):
    state = flow[...]
    for direction in range(4):
        products[direction] = dot(vol[direction], state)
    lifts[...] = jnp.zeros_like(lifts)
    pair[...] = jnp.zeros_like(pair)
    row = lax.broadcasted_iota(jnp.int32, (256, 1), 0).astype(F32).astype(BF16)
    for face in range(6):
        lifts[:, pl.ds(face * 128, NF)] = lift[face]
        other = sel[face ^ 1]
        cand[:, pl.ds(0, NE)] = dot(other, state).astype(BF16)
        width = NE
        if face < 4:
            cand[:, pl.ds(NE, HB)] = dot(other, heads[face]).astype(BF16)
            width = NE + HB
        place = nbr[pl.ds(face, 1), :]
        total = jnp.zeros((128, NE), F32)
        for start in range(0, width, 256):
            size = min(256, width - start)
            key = jnp.where((place >= start) & (place < start + size), place - start, -1)
            key = key.astype(F32).astype(BF16)
            chosen = jnp.where(row[:size] == key, jnp.ones((), BF16), jnp.zeros((), BF16))
            total = total + dot(cand[:, pl.ds(start, size)], chosen)
        pair[pl.ds(0, 128), :] = dot(sel[face], state).astype(BF16)
        pair[pl.ds(128, 128), :] = total.astype(BF16)
        mixes = []
        for side in range(2):
            wide = dot(spread[...], jac[face, side]).astype(BF16)
            wide = lax.dot_general(wide, spread[...], (((1,), (1,)), ((), ())), preferred_element_type=F32)
            mixes.append((wide * same[...]).astype(BF16))
        jumps[pl.ds(face * 128, 128), :] = dot(mixes[0], pair[pl.ds(0, 128), :]) + dot(mixes[1], pair[pl.ds(128, 128), :])


def solve_wall(wall, disp, resid, search, image, diag):
    T = 256
    lane = lax.broadcasted_iota(jnp.int32, (8, 128), 1)
    not_first = (lane != 0).astype(F32)
    not_last = (lane != 127).astype(F32)
    sub = lax.broadcasted_iota(jnp.int32, (8, 128), 0)
    zero = jnp.zeros((8, 128), F32)

    def total(acc):
        return jnp.sum(jnp.sum(acc, axis=0, keepdims=True), axis=1, keepdims=True)

    def start(c, acc):
        def body(t, acc):
            b = wall[c, 0, pl.ds(t, 8, stride=T), :]
            k = wall[c, 1, pl.ds(t, 8, stride=T), :]
            resid[c * T + t] = b
            diag[c * T + t] = 4.0 + k
            return acc + b * b

        return lax.fori_loop(0, T, body, acc, unroll=8)

    acc = zero
    for c in range(3):
        acc = start(c, acc)
    norm_now = total(acc)
    U = 8
    ratio = None
    for iteration in range(ITERS):
        first, last = iteration == 0, iteration == ITERS - 1

        def direction(i):
            if first:
                return resid[i]
            return resid[i] + ratio_b * search[i]

        if not first:
            ratio_b = jnp.broadcast_to(ratio, (8, 128))
        acc = zero
        for c in range(3):
            base = c * T
            top = direction(base)
            bottom = direction(base + T - 1)
            before = jnp.where(sub == 0, 0.0, pltpu.roll(bottom, 1, 0))
            beyond = jnp.where(sub == 7, 0.0, pltpu.roll(top, 7, 0))

            def one(t, above, here, below, acc):
                i = base + t
                beside = above + below + pltpu.roll(here, 1, 1) * not_first + pltpu.roll(here, 127, 1) * not_last
                value = diag[i] * here - beside
                if not last:
                    image[i] = value
                if not first:
                    search[i] = here
                return acc + here * value

            def block(b, carry):
                above, here, acc = carry
                for u in range(U):
                    t = b * U + u
                    below = direction(base + t + 1)
                    acc = one(t, above, here, below, acc)
                    above, here = here, below
                return above, here, acc

            above, here, acc = lax.fori_loop(0, T // U - 1, block, (before, top, acc))
            for t in range(T - U, T):
                below = beyond if t == T - 1 else direction(base + t + 1)
                acc = one(t, above, here, below, acc)
                above, here = here, below
        step = norm_now / total(acc)
        step_b = jnp.broadcast_to(step, (8, 128))

        def update(b, acc):
            for u in range(U):
                i = b * U + u
                r = resid[i]
                if first:
                    p = r
                    search[i] = r
                    disp[i] = step_b * p
                else:
                    p = search[i]
                    disp[i] = disp[i] + step_b * p
                if not last:
                    r = r - step_b * image[i]
                    resid[i] = r
                    acc = acc + r * r
            return acc

        acc = lax.fori_loop(0, 3 * T // U, update, zero)
        if not last:
            norm_next = total(acc)
            ratio = norm_next / norm_now
            norm_now = norm_next


def solve_kernel(
    anchor, wall, heads, flow, base, weight, nbr, vol, lift, jac, sel, spread, same,
    out, own_disp, disp, resid, search, image, diag, products, jumps, lifts, cand, pair, picked, flux,
):
    residual_parts(flow, heads, nbr, vol, lift, jac, sel, spread, same, products, jumps, lifts, cand, pair)
    solve_wall(wall, disp, resid, search, image, diag)
    sec, dom = lax.axis_index("sec"), lax.axis_index("dom")
    for c in range(3):
        for i in range(8):
            own_disp[c, pl.ds(i, 1), :] = disp[c * 256 + dom * 8 + i, pl.ds(sec, 1), :]
    lane = lax.broadcasted_iota(jnp.int32, (1, 128), 1)

    def pick(e, carry):
        a = anchor[e]
        line = a >> 7
        t, s, column = line & 255, line >> 8, a & 127
        hit = lane == column
        for c in range(3):
            value = disp[c * 256 + t, pl.ds(s, 1), :]
            picked[c, pl.ds(e, 1), :] = jnp.where(hit, value, 0.0)
        return carry

    lax.fori_loop(0, NE, pick, 0, unroll=8)
    ones = jnp.ones((8, 128), F32)
    geometry = []
    for k in range(4):
        row = base[pl.ds(k, 1), :]
        if k < 3:
            at = lax.dot_general(
                ones, picked[k], (((1,), (1,)), ((), ())), preferred_element_type=F32, precision=lax.Precision.HIGHEST
            )
            row = row * jnp.exp(weight[...] * at[:1])
        geometry.append(row)
    for face in range(6):
        rows = pl.ds(face * 128, 128)
        flux[rows, :] = (geometry[face // 2] * jumps[rows, :]).astype(BF16)
    total = dot(lifts[...], flux[...])
    for k in range(4):
        total = total + geometry[k] * products[k]
    out[...] = total.astype(BF16)


def on_device(flow_state, base_geometry, anchor_weight, wall_anchor, face_nbr, volume_ops, lift_ops, face_jac, wall_load, wall_stiff):
    wall, heads = exchange(wall_load, wall_stiff, flow_state)
    wall = wall.reshape(3, 2, 2048, 128)
    spread, same = expansion()
    vmem = pl.BlockSpec(memory_space=pltpu.VMEM)
    field = pltpu.VMEM((768, 8, 128), F32)
    return pl.pallas_call(
        solve_kernel,
        out_shape=(
            jax.ShapeDtypeStruct((NQ, NE), BF16),
            jax.ShapeDtypeStruct((3, 8, 128), F32),
        ),
        in_specs=[pl.BlockSpec(memory_space=pltpu.SMEM)] + [vmem] * 12,
        out_specs=(vmem, vmem),
        scratch_shapes=[
            field, field, field, field, field,
            pltpu.VMEM((4, NQ, NE), F32),
            pltpu.VMEM((768, NE), F32),
            pltpu.VMEM((NQ, 768), BF16),
            pltpu.VMEM((128, NE + HB), BF16),
            pltpu.VMEM((256, NE), BF16),
            pltpu.VMEM((3, NE, 128), F32),
            pltpu.VMEM((768, NE), BF16),
        ],
        compiler_params=pltpu.CompilerParams(vmem_limit_bytes=50 << 20),
        name="solve",
    )(
        wall_anchor, wall, heads, flow_state, base_geometry, anchor_weight.reshape(1, NE), face_nbr,
        volume_ops, lift_ops, face_jac,
        jnp.asarray(selection(), BF16), jnp.asarray(spread, BF16), jnp.asarray(same, F32),
    )


def solution(mesh):
    return jax.shard_map(
        on_device,
        mesh=mesh,
        in_specs=(
            P(None, ("sec", "dom")),
            P(None, ("sec", "dom")),
            P(("sec", "dom")),
            P(("sec", "dom")),
            P(None, ("sec", "dom")),
            P(),
            P(),
            P(),
            P(None, ("sec", "dom"), None),
            P(None, ("sec", "dom"), None),
        ),
        out_specs=(P(None, ("sec", "dom")), P(None, ("sec", "dom"), None)),
        check_vma=False,
    )
```

time: 1600 us -> 169 us (0.11)
  blocking collectives: 1250 us -> 0 us
  Pallas kernels: 0 us -> 153 us
  local copies, waits for them, and re-layouts: 120 us -> 14.8 us
  waiting for transfers between devices: 85.3 us -> 0 us
  starting transfers between devices: 60 us -> 0 us
  other arithmetic: 26.9 us -> 0 us
  matrix products: 25 us -> 0 us
  loops' own time: 16.5 us -> 0 us
    psum x17 -> x0, blocking collectives: 1250 us -> none  [the longest x9 667 us: squares(): return lax.psum(jnp.sum(resid * resid), ('sec', 'dom'))]
    pallas_call x0 -> x2, Pallas kernels: none -> 153 us  [the longest x1 104 us: on_device(): pl.pallas_call(solve_kernel, out_shape=(jax.ShapeDtypeStruct((NQ, NE), BF...]
    all_gather x1 -> x0, local copies, waits for them, and re-layouts: 60.6 us -> none  [on_device(): gathered = lax.all_gather(wall_disp, ('sec', 'dom'), axis=1, tiled=True)]
    ppermute x20 -> x0, starting transfers between devices: 59.9 us -> none  [the longest x8 38.4 us: padded_2(): after = lax.ppermute(leading, axis, down)]
    ppermute x20 -> x0, waiting for transfers between devices: 45.1 us -> none  [the longest x8 45 us: padded_2(): before = lax.ppermute(last, axis, up)]
    all_gather x1 -> x0, waiting for transfers between devices: 40.2 us -> none  [on_device(): gathered = lax.all_gather(wall_disp, ('sec', 'dom'), axis=1, tiled=True)]
    gather x7 -> x0, local copies, waits for them, and re-layouts: 35.4 us -> none  [the longest x6 24.9 us: on_device(): neighbour_trace = jnp.take(candidates, face_nbr[face], axis=1)]
    dot_general x16 -> x0, matrix products: 25 us -> none  [the longest x6 15.1 us: on_device(): jnp.dot(lift_ops[face], face_flux, preferred_element_type=jnp.float32)]
  transfers between devices with their start and end apart: 21 -> 0, of which waited for: 9 -> 0; matrix products, arithmetic and copies ran while one was open for 5% -> 0% of each run, Pallas kernels for 0% -> 0%
where the time goes in v1:
time: 169 us; the launch traced here: 168 us
  Pallas kernels  153 us (91%)
  local copies, waits for them, and re-layouts  14.8 us (9%)
    pallas_call x1, Pallas kernels, on_device(): pl.pallas_call(solve_kernel, out_shape=(jax.ShapeDtypeStruct((NQ, NE), BF...  104 us
    pallas_call x1, Pallas kernels, exchange(): pl.pallas_call(exchange_kernel, out_shape=(jax.ShapeDtypeStruct((3, 2, NY...  48.9 us
    unnamed x28, local copies, waits for them, and re-layouts  14.8 us

profile of v1, /device:TPU:1, one launch (start us, length us, event | category | flops | bytes accessed | tf_op | source)
XLA Modules:
  0.0 168.3 jit_solution(8212362026978517607)
XLA Ops:
  0.6 0.9 copy.16.jac
  1.5 1.3 copy.15.vol
  2.8 0.0 copy-start.1
  2.8 1.0 copy-done.1
  3.9 0.0 copy-start.9
  3.9 0.7 copy-done.9
  4.6 0.0 copy-start.10
  4.6 0.7 copy-done.10
  5.3 48.9 %exchange.1 = (f32[3,2,4,2,4,8,8,128]{7,6,5,4,3,2,1,0:T(8,128)S(1)}, bf16[4,270,128]{2,1,0:T(8,128)(2,1)S(1)}) custom-call(f32[3,8,128]{2,1,0:T(8,128)S(1)} %copy-done.9, f32[3,8,128]{2,1,0:T(8,128)S(1)} %copy-done.10, bf16[270,1024]{1,0:T(8,128)(2,1)S(1)} %copy-done.1), custom_call_target="tpu_custom_call" | custom-call | tf_op jit(solution)/shard_map/exchange/pallas_call | solution.py:196
  54.1 0.0 copy-start
  54.1 2.6 %copy-done = f32[3,2,4,2,4,8,8,128]{7,6,5,4,3,2,1,0:T(8,128)} copy-done((f32[3,2,4,2,4,8,8,128]{7,6,5,4,3,2,1,0:T(8,128)}, f32[3,2,4,2,4,8,8,128]{7,6,5,4,3,2,1,0:T(8,128)S(1)}, u32[]{:S(2)}) %copy-start) | copy-done | bytes 6291480
  56.8 0.0 copy-start.2
  56.8 1.1 copy-done.2
  57.8 0.0 copy-start.3
  57.8 1.1 copy-done.3
  58.9 0.0 copy-start.4
  58.9 1.0 copy-done.4
  59.9 0.0 copy-start.5
  59.9 0.8 copy-done.5
  60.7 0.0 copy-start.6
  60.7 0.8 copy-done.6
  61.5 0.0 copy-start.7
  61.5 0.8 copy-done.7
  62.3 0.0 copy-start.8
  62.3 0.7 copy-done.8
  63.0 0.0 copy-start.11
  63.0 0.7 copy-done.11
  63.7 0.0 copy-start.12
  63.7 0.7 copy-done.12
  64.4 104.0 %solve.1 = (bf16[270,1024]{1,0:T(8,128)(2,1)}, f32[3,8,128]{2,1,0:T(8,128)}) custom-call(s32[1024]{0:T(1024)S(1)} %copy-done.11, f32[3,2,2048,128]{3,2,1,0:T(8,128)} %bitcast.2, bf16[4,270,128]{2,1,0:T(8,128)(2,1)S(1)} %get-tuple-element.5.heads, bf16[270,1024]{1,0:T(8,128)(2,1)S(1)} %copy-done.2, f32[4,1024]{1,0:T(4,128)S(1)} %copy-done.8, ...), custom_call_target="tpu_custom_call" | custom-call | tf_op jit(solution)/shard_map/solve/pallas_call | solution.py:401
Async XLA Ops:
  2.8 1.1 copy-start.1
  3.9 0.7 copy-start.9
  4.6 0.7 copy-start.10
  54.1 2.6 %copy-start = (f32[3,2,4,2,4,8,8,128]{7,6,5,4,3,2,1,0:T(8,128)}, f32[3,2,4,2,4,8,8,128]{7,6,5,4,3,2,1,0:T(8,128)S(1)}, u32[]{:S(2)}) copy-start(f32[3,2,4,2,4,8,8,128]{7,6,5,4,3,2,1,0:T(8,128)S(1)} %get-tuple-element.4) | copy-start | bytes 18874372
  56.8 1.1 copy-start.2
  57.8 1.1 copy-start.3
  58.9 1.0 copy-start.4
  59.9 0.8 copy-start.5
  60.7 0.8 copy-start.6
  61.5 0.8 copy-start.7
  62.3 0.7 copy-start.8
  63.0 0.7 copy-start.11
  63.7 0.7 copy-start.12

commit v2 on v1

v2 whole, which is shorter than its diff:
```python
import jax
import jax.numpy as jnp
import numpy as np
from jax import lax
from jax.experimental import pallas as pl
from jax.experimental.pallas import tpu as pltpu
from jax.sharding import PartitionSpec as P

MESH = pl.DeviceIdType.MESH
ITERS = 8
NQ = 270
NF = 90
NE = 1024
HB = 128
NY, NC, NX, NZ = 4, 2, 4, 8
SIZE = {"y": NY, "x": NX, "z": NZ}
ORDERS = (("z", "x", "y"), ("x", "y", "z"), ("z", "y", "x"))
SLOTS = 16
T = 256
UNROLL = 64
F32 = jnp.float32
BF16 = jnp.bfloat16


def selection():
    index = np.arange(NQ).reshape(5, 2, 3, 3, 3)
    rows = np.zeros((6, 128, NQ), np.float32)
    for face in range(6):
        picked = np.take(index, 0 if face % 2 == 0 else 2, axis=2 + face // 2).reshape(-1)
        rows[face, np.arange(NF), picked] = 1.0
    return rows


def expansion():
    spread = np.zeros((128, 5), np.float32)
    spread[np.arange(NF), np.arange(NF) // 18] = 1.0
    same = np.zeros((128, 128), np.float32)
    inside = np.arange(NF)
    same[:NF, :NF] = inside[:, None] % 18 == inside[None, :] % 18
    return spread, same


def coordinates():
    sec, dom = lax.axis_index("sec"), lax.axis_index("dom")
    return {"y": sec // NC, "core": sec % NC, "x": dom // NZ, "z": dom % NZ}


def device(place):
    return (place["y"] * NC + place["core"], place["x"] * NZ + place["z"])


def moved(place, axis, by):
    size = SIZE[axis]
    return dict(place, **{axis: (place[axis] + by + size) % size})


class Gather:
    def __init__(self, color, here, wall, send, recv, pass_send, pass_recv):
        self.color, self.here, self.wall = color, here, wall
        self.send, self.recv = send, recv
        self.pass_send, self.pass_recv = pass_send, pass_recv
        self.order = ORDERS[color]
        self.rounds = 2 + SIZE[self.order[2]] // 2
        self.made, self.passed, self.used = [], [], 0

    def block(self, stage, axis, at, half):
        index = {}
        for name in "yxz":
            if name in self.order[:stage]:
                index[name] = slice(None)
            elif name == axis:
                index[name] = at
            else:
                index[name] = self.here[name]
        which = slice(None) if half is None else half
        core = self.here["core"]
        if isinstance(index["y"], slice):
            line = pl.ds(pl.multiple_of(core * NY, NY), NY)
        else:
            line = core * NY + index["y"]
        return self.wall.at[self.color, which, index["x"], index["z"], :, line]

    def copy(self, stage, axis, at, half, target, sems, slot):
        source = self.block(stage, axis, at, half)
        copy = pltpu.make_async_remote_copy(
            src_ref=source,
            dst_ref=source,
            send_sem=sems[0].at[slot],
            recv_sem=sems[1].at[slot],
            device_id=device(target),
            device_id_type=MESH,
        )
        copy.start()
        return copy

    def launch(self, number):
        copies = []
        if number < 2:
            axis = self.order[number]
            for by in sorted(range(1, SIZE[axis]), key=lambda by: -min(by, SIZE[axis] - by)):
                slot = self.color * SLOTS + self.used
                self.used += 1
                copies.append(
                    self.copy(
                        number, axis, self.here[axis], None, moved(self.here, axis, by), (self.send, self.recv), slot
                    )
                )
        else:
            axis, step = self.order[2], number - 2
            size = SIZE[axis]
            for way, sign in enumerate((1, -1)):
                half = None if step < size // 2 - 1 else way
                at = (self.here[axis] - sign * step + size) % size
                slot = self.color * SLOTS + self.used
                self.used += 1
                copies.append(
                    self.copy(2, axis, at, half, moved(self.here, axis, sign), (self.send, self.recv), slot)
                )
            if step == 0:
                self.hand_over(self.here[axis])
        self.made.append(copies)

    def hand_over(self, at):
        slot = self.color * NZ + len(self.passed)
        partner = dict(self.here, core=1 - self.here["core"])
        sems = (self.pass_send, self.pass_recv)
        self.passed.append(self.copy(2, self.order[2], at, None, partner, sems, slot))

    def advance(self, number):
        if number > self.rounds:
            return
        if number > 0:
            for copy in self.made[number - 1]:
                copy.wait_recv()
        if number < self.rounds:
            self.launch(number)
        if number > 2:
            axis, step = self.order[2], number - 3
            size = SIZE[axis]
            self.hand_over((self.here[axis] - step - 1 + size) % size)
            if step < size // 2 - 1:
                self.hand_over((self.here[axis] + step + 1) % size)

    def finish(self):
        for copies in self.made:
            for copy in copies:
                copy.wait_send()
        for copy in self.passed:
            copy.wait()


def dot(a, b):
    return jnp.dot(a, b, preferred_element_type=F32)


def volume_part(direction, flow, vol, products):
    products[direction] = dot(vol[direction], flow[...])


def face_part(face, flow, heads, nbr, jac, sel, spread, same, jumps, cand):
    state = flow[...]
    row = lax.broadcasted_iota(jnp.int32, (256, 1), 0).astype(F32).astype(BF16)
    other = sel[face ^ 1]
    cand[:, pl.ds(0, NE)] = dot(other, state).astype(BF16)
    width = NE
    if face < 4:
        cand[:, pl.ds(NE, HB)] = dot(other, heads[face]).astype(BF16)
        width = NE + HB
    place = nbr[pl.ds(face, 1), :]
    theirs = jnp.zeros((128, NE), F32)
    for start in range(0, width, 256):
        size = min(256, width - start)
        key = jnp.where((place >= start) & (place < start + size), place - start, -1)
        key = key.astype(F32).astype(BF16)
        chosen = jnp.where(row[:size] == key, jnp.ones((), BF16), jnp.zeros((), BF16))
        theirs = theirs + dot(cand[:, pl.ds(start, size)], chosen)
    mine = dot(sel[face], state)
    mixes = []
    for side in range(2):
        wide = dot(spread[...], jac[face, side]).astype(BF16)
        wide = lax.dot_general(wide, spread[...], (((1,), (1,)), ((), ())), preferred_element_type=F32)
        mixes.append((wide * same[...]).astype(BF16))
    jumps[pl.ds(face * 128, 128), :] = dot(mixes[0], mine.astype(BF16)) + dot(mixes[1], theirs.astype(BF16))


def exchange_kernel(
    load, stiff, flow_in, nbr_in, vol_in, lift_in, jac_in, sel_in, spread_in, same_in,
    wall, products, jumps, lifts,
    heads, flow, nbr, vol, lift, jac, sel, spread, same, cand,
    send, recv, pass_send, pass_recv, head_send, head_recv, in_sem,
):
    here = coordinates()
    sec, dom = lax.axis_index("sec"), lax.axis_index("dom")
    n_sec, n_dom = NY * NC, NX * NZ
    sides = [
        (sec, (dom + 1) % n_dom),
        (sec, (dom + n_dom - 1) % n_dom),
        ((sec + 1) % n_sec, dom),
        ((sec + n_sec - 1) % n_sec, dom),
    ]
    peers = list(sides)
    for axis in "yxz":
        for by in range(1, SIZE[axis]):
            peers.append(device(moved(here, axis, by)))
    peers.append(device(dict(here, core=1 - here["core"])))
    barrier = pltpu.get_barrier_semaphore()
    for peer in peers:
        pl.semaphore_signal(barrier, inc=1, device_id=peer, device_id_type=MESH)
    line = here["core"] * NY + here["y"]
    pairs = [
        (load, wall.at[:, 0, here["x"], here["z"], :, line]),
        (stiff, wall.at[:, 1, here["x"], here["z"], :, line]),
        (flow_in, flow), (vol_in, vol), (nbr_in, nbr), (jac_in, jac),
        (sel_in, sel), (spread_in, spread), (same_in, same), (lift_in, lift),
    ]
    local = [pltpu.make_async_copy(a, b, in_sem.at[i]) for i, (a, b) in enumerate(pairs)]
    for copy in local:
        copy.start()
    lifts[...] = jnp.zeros_like(lifts)
    local[0].wait()
    local[1].wait()
    pl.semaphore_wait(barrier, len(peers))
    gathers = [Gather(color, here, wall, send, recv, pass_send, pass_recv) for color in range(3)]

    def advance(number):
        for gather in gathers:
            gather.advance(number)

    advance(0)
    head_copies = []
    for face, peer in enumerate(sides):
        copy = pltpu.make_async_remote_copy(
            src_ref=flow_in.at[:, pl.ds(0, HB)],
            dst_ref=heads.at[face],
            send_sem=head_send.at[face],
            recv_sem=head_recv.at[face],
            device_id=peer,
            device_id_type=MESH,
        )
        copy.start()
        head_copies.append(copy)
    for copy in local[2:]:
        copy.wait()

    def face(number):
        face_part(number, flow, heads, nbr, jac, sel, spread, same, jumps, cand)

    for direction in range(4):
        volume_part(direction, flow, vol, products)
    advance(1)
    for number in range(6):
        lifts[:, pl.ds(number * 128, NF)] = lift[number]
    face(4)
    face(5)
    advance(2)
    for copy in head_copies:
        copy.wait()
    face(0)
    advance(3)
    face(1)
    face(2)
    advance(4)
    face(3)
    advance(5)
    advance(6)
    for gather in gathers:
        gather.finish()


def stay(x):
    return pltpu.with_memory_space_constraint(x, pltpu.HBM)


def exchange(wall_load, wall_stiff, flow_state, face_nbr, volume_ops, lift_ops, face_jac):
    vmem = pl.BlockSpec(memory_space=pltpu.VMEM)
    far = pl.BlockSpec(memory_space=pltpu.HBM)
    spread, same = expansion()
    dma = pltpu.SemaphoreType.DMA
    return pl.pallas_call(
        exchange_kernel,
        out_shape=(
            jax.ShapeDtypeStruct((3, 2, NX, NZ, 8, NC * NY, 128), F32),
            jax.ShapeDtypeStruct((4, NQ, NE), F32),
            jax.ShapeDtypeStruct((768, NE), F32),
            jax.ShapeDtypeStruct((NQ, 768), BF16),
        ),
        in_specs=[far] * 10,
        out_specs=(vmem,) * 4,
        scratch_shapes=[
            pltpu.VMEM((4, NQ, HB), BF16),
            pltpu.VMEM((NQ, NE), BF16),
            pltpu.VMEM((6, NE), jnp.int32),
            pltpu.VMEM((4, NQ, NQ), BF16),
            pltpu.VMEM((6, NQ, NF), BF16),
            pltpu.VMEM((6, 2, 5, 5), BF16),
            pltpu.VMEM((6, 128, NQ), BF16),
            pltpu.VMEM((128, 5), BF16),
            pltpu.VMEM((128, 128), F32),
            pltpu.VMEM((128, NE + HB), BF16),
            dma((3 * SLOTS,)),
            dma((3 * SLOTS,)),
            dma((3 * NZ,)),
            dma((3 * NZ,)),
            dma((4,)),
            dma((4,)),
            dma((10,)),
        ],
        compiler_params=pltpu.CompilerParams(collective_id=0, has_side_effects=True, vmem_limit_bytes=32 << 20),
        name="exchange",
    )(
        *map(
            stay,
            (
                wall_load, wall_stiff, flow_state, face_nbr, volume_ops, lift_ops, face_jac,
                jnp.asarray(selection(), BF16), jnp.asarray(spread, BF16), jnp.asarray(same, F32),
            ),
        )
    )


def rows(i):
    return pl.ds(pl.multiple_of(i * 8, 8), 8)


def solve_wall(wall, disp, resid, searches, image, diag):
    lane = lax.broadcasted_iota(jnp.int32, (8, 128), 1)
    sub = lax.broadcasted_iota(jnp.int32, (8, 128), 0)
    zero = jnp.zeros((8, 128), F32)

    def total(acc):
        return jnp.sum(jnp.sum(acc, axis=0, keepdims=True), axis=1, keepdims=True)

    def previous(v):
        return jnp.where(sub >= 4, pltpu.roll(v, 4, 0), jnp.where(sub == 0, 0.0, pltpu.roll(v, 5, 0)))

    def following(v):
        return jnp.where(sub < 4, pltpu.roll(v, 4, 0), jnp.where(sub == 7, 0.0, pltpu.roll(v, 3, 0)))

    ratio = norm_now = None
    steps = []
    for iteration in range(ITERS):
        first, last = iteration == 0, iteration == ITERS - 1
        old, new = searches[(iteration + 1) % 2], searches[iteration % 2]
        if not first:
            ratio_b = jnp.broadcast_to(ratio, (8, 128))

        def direction(c, t):
            if first:
                return wall[c, 0, rows(t), :]
            return resid[rows(c * T + t), :] + ratio_b * old[rows(c * T + t), :]

        sums = (zero, zero)
        norms = (zero, zero)
        for c in range(3):
            top, bottom = direction(c, 0), direction(c, T - 1)

            def one(t, above, here, below, sums, norms):
                i = rows(c * T + t)
                left = jnp.where(lane == 0, 0.0, pltpu.roll(here, 1, 1))
                right = jnp.where(lane == 127, 0.0, pltpu.roll(here, 127, 1))
                if first:
                    middle = 4.0 + wall[c, 1, rows(t), :]
                    diag[i, :] = middle
                    norms = (norms[1], norms[0] + here * here)
                else:
                    middle = diag[i, :]
                value = middle * here - ((above + below) + (left + right))
                if not last:
                    image[i, :] = value
                new[i, :] = here
                return (sums[1], sums[0] + here * value), norms

            def block(b, carry, ends=False):
                above, here, sums, norms = carry
                for u in range(UNROLL):
                    t = b * UNROLL + u
                    if ends and u == UNROLL - 1:
                        below = following(top)
                    else:
                        below = direction(c, t + 1)
                    sums, norms = one(t, above, here, below, sums, norms)
                    above, here = here, below
                return above, here, sums, norms

            carry = (previous(bottom), top, sums, norms)
            carry = lax.fori_loop(0, T // UNROLL - 1, block, carry)
            _, _, sums, norms = block(T // UNROLL - 1, carry, ends=True)
        if first:
            norm_now = total(norms[0] + norms[1])
        step = jnp.broadcast_to(norm_now / total(sums[0] + sums[1]), (8, 128))
        steps.append(step)
        if first:
            source = [wall.at[c, 0] for c in range(3)]
        else:
            source = None

        def update(b, norms, c=None):
            for u in range(UNROLL // 2):
                t = b * (UNROLL // 2) + u
                i = rows(t if c is None else c * T + t)
                if iteration % 2 == 1:
                    gain = steps[iteration - 1] * old[i, :] + step * new[i, :]
                    disp[i, :] = gain if iteration == 1 else disp[i, :] + gain
                if not last:
                    held = source[c][rows(t), :] if first else resid[i, :]
                    held = held - step * image[i, :]
                    resid[i, :] = held
                    norms = (norms[1], norms[0] + held * held)
            return norms

        norms = (zero, zero)
        if first:
            for c in range(3):
                norms = lax.fori_loop(0, 2 * T // UNROLL, lambda b, n, c=c: update(b, n, c), norms)
        else:
            norms = lax.fori_loop(0, 6 * T // UNROLL, update, norms)
        if not last:
            norm_next = total(norms[0] + norms[1])
            ratio = norm_next / norm_now
            norm_now = norm_next


def solve_kernel(
    anchor_in, base_in, weight_in, wall, products, jumps, lifts,
    out, own_disp,
    disp, resid, search_a, search_b, image, diag, picked, flux, anchor, base, weight, in_sem,
):
    pairs = [(anchor_in, anchor), (base_in, base), (weight_in, weight)]
    local = [pltpu.make_async_copy(a, b, in_sem.at[i]) for i, (a, b) in enumerate(pairs)]
    for copy in local:
        copy.start()
    for copy in local:
        copy.wait()
    solve_wall(wall, disp, resid, (search_a, search_b), image, diag)
    sec, dom = lax.axis_index("sec"), lax.axis_index("dom")
    line = (sec % NC) * NY + sec // NC
    for c in range(3):
        for i in range(8):
            own_disp[c, pl.ds(i, 1), :] = disp[pl.ds((c * T + dom * 8 + i) * 8 + line, 1), :]
    lane = lax.broadcasted_iota(jnp.int32, (1, 128), 1)

    def pick(e, carry):
        a = anchor[e]
        s = a >> 15
        at = ((a >> 7) & (T - 1)) * 8 + (s & 1) * NY + (s >> 1)
        hit = lane == (a & 127)
        for c in range(3):
            picked[c, pl.ds(e, 1), :] = jnp.where(hit, disp[pl.ds(c * T * 8 + at, 1), :], 0.0)
        return carry

    lax.fori_loop(0, NE, pick, 0, unroll=16)
    ones = jnp.ones((8, 128), F32)
    geometry = []
    for k in range(4):
        row = base[pl.ds(k, 1), :]
        if k < 3:
            at = lax.dot_general(
                ones, picked[k], (((1,), (1,)), ((), ())), preferred_element_type=F32, precision=lax.Precision.HIGHEST
            )
            row = row * jnp.exp(weight[...] * at[:1])
        geometry.append(row)
    for face in range(6):
        at = pl.ds(face * 128, 128)
        flux[at, :] = (geometry[face // 2] * jumps[at, :]).astype(BF16)
    result = dot(lifts[...], flux[...])
    for k in range(4):
        result = result + geometry[k] * products[k]
    out[...] = result.astype(BF16)


def on_device(
    flow_state, base_geometry, anchor_weight, wall_anchor, face_nbr, volume_ops, lift_ops, face_jac, wall_load, wall_stiff
):
    wall, products, jumps, lifts = exchange(
        wall_load, wall_stiff, flow_state, face_nbr, volume_ops, lift_ops, face_jac
    )
    wall = wall.reshape(3, 2, T * 8, 128)
    vmem = pl.BlockSpec(memory_space=pltpu.VMEM)
    far = pl.BlockSpec(memory_space=pltpu.HBM)
    field = pltpu.VMEM((3 * T * 8, 128), F32)
    return pl.pallas_call(
        solve_kernel,
        out_shape=(
            jax.ShapeDtypeStruct((NQ, NE), BF16),
            jax.ShapeDtypeStruct((3, 8, 128), F32),
        ),
        in_specs=[far] * 3 + [vmem] * 4,
        out_specs=(vmem, vmem),
        scratch_shapes=[field] * 6
        + [
            pltpu.VMEM((3, NE, 128), F32),
            pltpu.VMEM((768, NE), BF16),
            pltpu.SMEM((NE,), jnp.int32),
            pltpu.VMEM((4, NE), F32),
            pltpu.VMEM((1, NE), F32),
            pltpu.SemaphoreType.DMA((3,)),
        ],
        compiler_params=pltpu.CompilerParams(vmem_limit_bytes=28 << 20),
        name="solve",
    )(
        *map(stay, (wall_anchor, base_geometry, anchor_weight.reshape(1, NE))), wall, products, jumps, lifts
    )


def solution(mesh):
    return jax.shard_map(
        on_device,
        mesh=mesh,
        in_specs=(
            P(None, ("sec", "dom")),
            P(None, ("sec", "dom")),
            P(("sec", "dom")),
            P(("sec", "dom")),
            P(None, ("sec", "dom")),
            P(),
            P(),
            P(),
            P(None, ("sec", "dom"), None),
            P(None, ("sec", "dom"), None),
        ),
        out_specs=(P(None, ("sec", "dom")), P(None, ("sec", "dom"), None)),
        check_vma=False,
    )
```

time: 169 us -> 83.4 us (0.49)
  Pallas kernels: 153 us -> 78.6 us
  local copies, waits for them, and re-layouts: 14.8 us -> 3.67 us
    pallas_call x1, Pallas kernels: 104 us -> 35.2 us  [on_device(): pl.pallas_call(solve_kernel, out_shape=(jax.ShapeDtypeStruct((NQ, NE), BF...]
    unnamed x28 -> x2, local copies, waits for them, and re-layouts: 14.8 us -> 3.67 us
    pallas_call x1, Pallas kernels: 48.9 us -> 43.5 us  [exchange(): pl.pallas_call(exchange_kernel, out_shape=(jax.ShapeDtypeStruct((3, 2, NX...]
where the time goes in v2:
time: 83.4 us; the launch traced here: 83.1 us
  Pallas kernels  78.6 us (94%)
  local copies, waits for them, and re-layouts  3.67 us (4%)
    pallas_call x1, Pallas kernels, exchange(): pl.pallas_call(exchange_kernel, out_shape=(jax.ShapeDtypeStruct((3, 2, NX...  43.5 us
    pallas_call x1, Pallas kernels, on_device(): pl.pallas_call(solve_kernel, out_shape=(jax.ShapeDtypeStruct((NQ, NE), BF...  35.2 us
    unnamed x2, local copies, waits for them, and re-layouts  3.67 us

profile of v2, /device:TPU:1, one launch (start us, length us, event | category | flops | bytes accessed | tf_op | source)
XLA Modules:
  0.0 83.1 jit_solution(526733673568264822)
XLA Ops:
  0.6 1.5 %copy.16.jac_in = bf16[6,2,5,5]{3,2,1,0:T(8,128)(2,1)} copy(bf16[6,2,5,5]{0,1,3,2:T(2,128)(2,1)} %param.20) | data formatting | bytes 1200 | tf_op args[7]
  2.1 2.2 %copy.15.vol_in = bf16[4,270,270]{2,1,0:T(8,128)(2,1)} copy(bf16[4,270,270]{2,0,1:T(4,128)(2,1)} %param.18) | data formatting | bytes 1166400 | tf_op args[5]
  4.3 43.5 %exchange.1 = (f32[3,2,4,8,8,8,128]{6,5,4,3,2,1,0:T(8,128)S(1)}, f32[4,270,1024]{2,1,0:T(8,128)S(1)}, f32[768,1024]{1,0:T(8,128)S(1)}, bf16[270,768]{1,0:T(8,128)(2,1)S(1)}) custom-call(f32[3,8,128]{2,1,0:T(8,128)} %load.1, f32[3,8,128]{2,1,0:T(8,128)} %stiff.1, bf16[270,1024]{1,0:T(8,128)(2,1)} %flow_in.1, s32[6,1024]{1,0:T(8,128)} %nbr_in.1, ...), custom_call_target="tpu_custom_call" | custom-call | tf_op jit(solution)/shard_map/exchange/pallas_call | solution.py:279
  47.8 35.2 %solve.1 = (bf16[270,1024]{1,0:T(8,128)(2,1)}, f32[3,8,128]{2,1,0:T(8,128)}) custom-call(s32[1024]{0:T(1024)} %anchor_in.1, f32[4,1024]{1,0:T(4,128)} %base_in.1, f32[1,1024]{1,0:T(1,128)} %bitcast.3, f32[3,2,2048,128]{3,2,1,0:T(8,128)S(1)} %bitcast.2, f32[4,270,1024]{2,1,0:T(8,128)S(1)} %get-tuple-element.7.products, ...), custom_call_target="tpu_custom_call" | custom-call | tf_op jit(solution)/shard_map/solve/pallas_call | solution.py:481

commit v3 on v2

--- a/solution.py
+++ b/solution.py
@@ -15,9 +15,10 @@
 NY, NC, NX, NZ = 4, 2, 4, 8
 SIZE = {"y": NY, "x": NX, "z": NZ}
 ORDERS = (("z", "x", "y"), ("x", "y", "z"), ("z", "y", "x"))
-SLOTS = 16
+SLOTS = 24
 T = 256
 UNROLL = 64
+STIFF_LOW, STIFF_UNIT = 0.01, 0.29 / 65535.0
 F32 = jnp.float32
 BF16 = jnp.bfloat16
 
@@ -57,11 +58,13 @@
 class Gather:
     def __init__(self, color, here, wall, send, recv, pass_send, pass_recv):
         self.color, self.here, self.wall = color, here, wall
-        self.send, self.recv = send, recv
-        self.pass_send, self.pass_recv = pass_send, pass_recv
+        self.sems, self.pass_sems = (send, recv), (pass_send, pass_recv)
         self.order = ORDERS[color]
-        self.rounds = 2 + SIZE[self.order[2]] // 2
-        self.made, self.passed, self.used = [], [], 0
+        self.size = SIZE[self.order[2]]
+        self.reach = self.size // 2
+        self.events = 4 + 2 * (self.reach - 1)
+        self.lines, self.ring, self.passed = [[], []], {}, []
+        self.used = 0
 
     def block(self, stage, axis, at, half):
         index = {}
@@ -72,13 +75,15 @@
                 index[name] = at
             else:
                 index[name] = self.here[name]
-        which = slice(None) if half is None else half
+        if half is not None:
+            cut = "x" if axis != "x" else "z"
+            index[cut] = pl.ds(half * (SIZE[cut] // 2), SIZE[cut] // 2)
         core = self.here["core"]
         if isinstance(index["y"], slice):
             line = pl.ds(pl.multiple_of(core * NY, NY), NY)
         else:
             line = core * NY + index["y"]
-        return self.wall.at[self.color, which, index["x"], index["z"], :, line]
+        return self.wall.at[self.color, index["x"], index["z"], :, line]
 
     def copy(self, stage, axis, at, half, target, sems, slot):
         source = self.block(stage, axis, at, half)
@@ -93,64 +98,88 @@
         copy.start()
         return copy
 
-    def launch(self, number):
-        copies = []
-        if number < 2:
-            axis = self.order[number]
-            for by in sorted(range(1, SIZE[axis]), key=lambda by: -min(by, SIZE[axis] - by)):
-                slot = self.color * SLOTS + self.used
-                self.used += 1
-                copies.append(
-                    self.copy(
-                        number, axis, self.here[axis], None, moved(self.here, axis, by), (self.send, self.recv), slot
-                    )
-                )
+    def slot(self):
+        self.used += 1
+        return self.color * SLOTS + self.used - 1
+
+    def launch_line(self, number):
+        axis = self.order[number]
+        for by in sorted(range(1, SIZE[axis]), key=lambda by: -min(by, SIZE[axis] - by)):
+            target = moved(self.here, axis, by)
+            self.lines[number].append(
+                self.copy(number, axis, self.here[axis], None, target, self.sems, self.slot())
+            )
+
+    def around(self, by):
+        return (self.here[self.order[2]] + by + self.size) % self.size
+
+    def launch_ring(self, step, half):
+        for way, sign in enumerate((1, -1)):
+            if step == self.reach - 1 and way != half:
+                continue
+            target = moved(self.here, self.order[2], sign)
+            self.ring[step, half, way] = self.copy(
+                2, self.order[2], self.around(-sign * step), half, target, self.sems, self.slot()
+            )
+
+    def hand_over(self, by, half):
+        slot = self.color * 2 * NZ + len(self.passed)
+        partner = dict(self.here, core=1 - self.here["core"])
+        self.passed.append(self.copy(2, self.order[2], self.around(by), half, partner, self.pass_sems, slot))
+
+    def advance(self, event):
+        if event >= self.events:
+            return
+        if event < 2:
+            if event == 1:
+                for copy in self.lines[0]:
+                    copy.wait_recv()
+            self.launch_line(event)
+        elif event == 2:
+            for copy in self.lines[1]:
+                copy.wait_recv()
+            self.launch_ring(0, 0)
+            self.launch_ring(0, 1)
+            self.hand_over(0, 0)
+            self.hand_over(0, 1)
+        elif event < self.events - 1:
+            step, half = (event - 3) // 2 + 1, (event - 3) % 2
+            for way in range(2):
+                self.ring[step - 1, half, way].wait_recv()
+            self.launch_ring(step, half)
+            self.hand_over(-step, half)
+            self.hand_over(step, half)
         else:
-            axis, step = self.order[2], number - 2
-            size = SIZE[axis]
-            for way, sign in enumerate((1, -1)):
-                half = None if step < size // 2 - 1 else way
-                at = (self.here[axis] - sign * step + size) % size
-                slot = self.color * SLOTS + self.used
-                self.used += 1
-                copies.append(
-                    self.copy(2, axis, at, half, moved(self.here, axis, sign), (self.send, self.recv), slot)
-                )
-            if step == 0:
-                self.hand_over(self.here[axis])
-        self.made.append(copies)
-
-    def hand_over(self, at):
-        slot = self.color * NZ + len(self.passed)
-        partner = dict(self.here, core=1 - self.here["core"])
-        sems = (self.pass_send, self.pass_recv)
-        self.passed.append(self.copy(2, self.order[2], at, None, partner, sems, slot))
-
-    def advance(self, number):
-        if number > self.rounds:
-            return
-        if number > 0:
-            for copy in self.made[number - 1]:
-                copy.wait_recv()
-        if number < self.rounds:
-            self.launch(number)
-        if number > 2:
-            axis, step = self.order[2], number - 3
-            size = SIZE[axis]
-            self.hand_over((self.here[axis] - step - 1 + size) % size)
-            if step < size // 2 - 1:
-                self.hand_over((self.here[axis] + step + 1) % size)
+            for half in range(2):
+                self.ring[self.reach - 1, half, half].wait_recv()
+                self.hand_over(self.reach, half)
 
     def finish(self):
-        for copies in self.made:
-            for copy in copies:
-                copy.wait_send()
+        for copy in self.lines[0] + self.lines[1] + list(self.ring.values()):
+            copy.wait_send()
         for copy in self.passed:
             copy.wait()
 
 
 def dot(a, b):
     return jnp.dot(a, b, preferred_element_type=F32)
+
+
+def pack_wall(load, stiff, out):
+    largest = jnp.max(jnp.max(jnp.abs(load), axis=0, keepdims=True), axis=1, keepdims=True)
+    power = jnp.ceil(jnp.log2(jnp.maximum(largest, 1e-30)) + 1e-4)
+    power = jnp.broadcast_to(power, (1, 128)).astype(jnp.int32)
+    unit = load_unit(power)
+    high = jnp.clip(jnp.round(load / unit), -32767.0, 32767.0).astype(jnp.int32)
+    low = jnp.clip(jnp.round((stiff - STIFF_LOW) / STIFF_UNIT), 0.0, 65535.0).astype(jnp.int32)
+    word = (high << 16) | low
+    for i in range(8):
+        out[pl.ds(i, 1), :] = word[i : i + 1]
+    out[pl.ds(8, 1), :] = power
+
+
+def load_unit(power):
+    return jnp.exp2(power.astype(F32)) * (1.0 / 32767.0)
 
 
 def volume_part(direction, flow, vol, products):
@@ -184,9 +213,9 @@
 
 
 def exchange_kernel(
-    load, stiff, flow_in, nbr_in, vol_in, lift_in, jac_in, sel_in, spread_in, same_in,
+    load, stiff, flow_in, nbr_in, vol, lift_in, jac, sel_in, spread_in, same_in,
     wall, products, jumps, lifts,
-    heads, flow, nbr, vol, lift, jac, sel, spread, same, cand,
+    heads, flow, nbr, lift, sel, spread, same, cand, own_load, own_stiff,
     send, recv, pass_send, pass_recv, head_send, head_recv, in_sem,
 ):
     here = coordinates()
@@ -206,27 +235,33 @@
     barrier = pltpu.get_barrier_semaphore()
     for peer in peers:
         pl.semaphore_signal(barrier, inc=1, device_id=peer, device_id_type=MESH)
-    line = here["core"] * NY + here["y"]
     pairs = [
-        (load, wall.at[:, 0, here["x"], here["z"], :, line]),
-        (stiff, wall.at[:, 1, here["x"], here["z"], :, line]),
-        (flow_in, flow), (vol_in, vol), (nbr_in, nbr), (jac_in, jac),
+        (load, own_load), (stiff, own_stiff), (flow_in, flow), (nbr_in, nbr),
         (sel_in, sel), (spread_in, spread), (same_in, same), (lift_in, lift),
     ]
     local = [pltpu.make_async_copy(a, b, in_sem.at[i]) for i, (a, b) in enumerate(pairs)]
     for copy in local:
         copy.start()
-    lifts[...] = jnp.zeros_like(lifts)
     local[0].wait()
     local[1].wait()
+    line = here["core"] * NY + here["y"]
+    for c in range(3):
+        pack_wall(own_load[c], own_stiff[c], wall.at[c, here["x"], here["z"], :, line])
+    lifts[...] = jnp.zeros_like(lifts)
     pl.semaphore_wait(barrier, len(peers))
     gathers = [Gather(color, here, wall, send, recv, pass_send, pass_recv) for color in range(3)]
 
-    def advance(number):
-        for gather in gathers:
-            gather.advance(number)
+    def advance(*events):
+        for event in events:
+            for gather in gathers:
+                gather.advance(event)
 
     advance(0)
+    for copy in local[2:]:
+        copy.wait()
+    for direction in range(4):
+        volume_part(direction, flow, vol, products)
+    advance(1)
     head_copies = []
     for face, peer in enumerate(sides):
         copy = pltpu.make_async_remote_copy(
@@ -239,15 +274,10 @@
         )
         copy.start()
         head_copies.append(copy)
-    for copy in local[2:]:
-        copy.wait()
 
     def face(number):
         face_part(number, flow, heads, nbr, jac, sel, spread, same, jumps, cand)
 
-    for direction in range(4):
-        volume_part(direction, flow, vol, products)
-    advance(1)
     for number in range(6):
         lifts[:, pl.ds(number * 128, NF)] = lift[number]
     face(4)
@@ -258,11 +288,11 @@
     face(0)
     advance(3)
     face(1)
+    advance(4)
     face(2)
-    advance(4)
+    advance(5, 6)
     face(3)
-    advance(5)
-    advance(6)
+    advance(7, 8, 9)
     for gather in gathers:
         gather.finish()
 
@@ -279,42 +309,40 @@
     return pl.pallas_call(
         exchange_kernel,
         out_shape=(
-            jax.ShapeDtypeStruct((3, 2, NX, NZ, 8, NC * NY, 128), F32),
+            jax.ShapeDtypeStruct((3, NX, NZ, 9, NC * NY, 128), jnp.int32),
             jax.ShapeDtypeStruct((4, NQ, NE), F32),
             jax.ShapeDtypeStruct((768, NE), F32),
             jax.ShapeDtypeStruct((NQ, 768), BF16),
         ),
-        in_specs=[far] * 10,
+        in_specs=[far] * 4 + [vmem, far, vmem] + [far] * 3,
         out_specs=(vmem,) * 4,
         scratch_shapes=[
             pltpu.VMEM((4, NQ, HB), BF16),
             pltpu.VMEM((NQ, NE), BF16),
             pltpu.VMEM((6, NE), jnp.int32),
-            pltpu.VMEM((4, NQ, NQ), BF16),
             pltpu.VMEM((6, NQ, NF), BF16),
-            pltpu.VMEM((6, 2, 5, 5), BF16),
             pltpu.VMEM((6, 128, NQ), BF16),
             pltpu.VMEM((128, 5), BF16),
             pltpu.VMEM((128, 128), F32),
             pltpu.VMEM((128, NE + HB), BF16),
+            pltpu.VMEM((3, 8, 128), F32),
+            pltpu.VMEM((3, 8, 128), F32),
             dma((3 * SLOTS,)),
             dma((3 * SLOTS,)),
-            dma((3 * NZ,)),
-            dma((3 * NZ,)),
+            dma((3 * 2 * NZ,)),
+            dma((3 * 2 * NZ,)),
             dma((4,)),
             dma((4,)),
-            dma((10,)),
+            dma((8,)),
         ],
         compiler_params=pltpu.CompilerParams(collective_id=0, has_side_effects=True, vmem_limit_bytes=32 << 20),
         name="exchange",
     )(
-        *map(
-            stay,
-            (
-                wall_load, wall_stiff, flow_state, face_nbr, volume_ops, lift_ops, face_jac,
-                jnp.asarray(selection(), BF16), jnp.asarray(spread, BF16), jnp.asarray(same, F32),
-            ),
-        )
+        *map(stay, (wall_load, wall_stiff, flow_state, face_nbr)),
+        volume_ops,
+        stay(lift_ops),
+        face_jac,
+        *map(stay, (jnp.asarray(selection(), BF16), jnp.asarray(spread, BF16), jnp.asarray(same, F32))),
     )
 
 
@@ -344,22 +372,34 @@
         if not first:
             ratio_b = jnp.broadcast_to(ratio, (8, 128))
 
-        def direction(c, t):
-            if first:
-                return wall[c, 0, rows(t), :]
-            return resid[rows(c * T + t), :] + ratio_b * old[rows(c * T + t), :]
+        def direction(c, b, u):
+            if not first:
+                i = rows(c * T + b * UNROLL + u)
+                return resid[i, :] + ratio_b * old[i, :]
+            group = (c * T + b * UNROLL) // 8 + u // 8
+            if (c, u // 8) not in units:
+                units[c, u // 8] = load_unit(wall[rows(group * 9 + 8), :])
+            return (wall[rows(group * 9 + u % 8), :] >> 16).astype(F32) * units[c, u // 8]
+
+        def stiffness(c, b, u):
+            group = (c * T + b * UNROLL) // 8 + u // 8
+            code = wall[rows(group * 9 + u % 8), :] & 65535
+            return (4.0 + STIFF_LOW) + code.astype(F32) * STIFF_UNIT
 
         sums = (zero, zero)
         norms = (zero, zero)
         for c in range(3):
-            top, bottom = direction(c, 0), direction(c, T - 1)
-
-            def one(t, above, here, below, sums, norms):
-                i = rows(c * T + t)
+            units = {}
+            top = direction(c, 0, 0)
+            units = {}
+            bottom = direction(c, T // UNROLL - 1, UNROLL - 1)
+
+            def one(b, u, above, here, below, sums, norms):
+                i = rows(c * T + b * UNROLL + u)
                 left = jnp.where(lane == 0, 0.0, pltpu.roll(here, 1, 1))
                 right = jnp.where(lane == 127, 0.0, pltpu.roll(here, 127, 1))
                 if first:
-                    middle = 4.0 + wall[c, 1, rows(t), :]
+                    middle = stiffness(c, b, u)
                     diag[i, :] = middle
                     norms = (norms[1], norms[0] + here * here)
                 else:
@@ -372,13 +412,13 @@
 
             def block(b, carry, ends=False):
                 above, here, sums, norms = carry
+                units.clear()
                 for u in range(UNROLL):
-                    t = b * UNROLL + u
                     if ends and u == UNROLL - 1:
                         below = following(top)
                     else:
-                        below = direction(c, t + 1)
-                    sums, norms = one(t, above, here, below, sums, norms)
+                        below = direction(c, b, u + 1)
+                    sums, norms = one(b, u, above, here, below, sums, norms)
                     above, here = here, below
                 return above, here, sums, norms
 
@@ -389,31 +429,20 @@
             norm_now = total(norms[0] + norms[1])
         step = jnp.broadcast_to(norm_now / total(sums[0] + sums[1]), (8, 128))
         steps.append(step)
-        if first:
-            source = [wall.at[c, 0] for c in range(3)]
-        else:
-            source = None
-
-        def update(b, norms, c=None):
+        def update(b, norms):
             for u in range(UNROLL // 2):
-                t = b * (UNROLL // 2) + u
-                i = rows(t if c is None else c * T + t)
+                i = rows(b * (UNROLL // 2) + u)
                 if iteration % 2 == 1:
                     gain = steps[iteration - 1] * old[i, :] + step * new[i, :]
                     disp[i, :] = gain if iteration == 1 else disp[i, :] + gain
                 if not last:
-                    held = source[c][rows(t), :] if first else resid[i, :]
-                    held = held - step * image[i, :]
+                    held = (new if first else resid)[i, :] - step * image[i, :]
                     resid[i, :] = held
                     norms = (norms[1], norms[0] + held * held)
             return norms
 
         norms = (zero, zero)
-        if first:
-            for c in range(3):
-                norms = lax.fori_loop(0, 2 * T // UNROLL, lambda b, n, c=c: update(b, n, c), norms)
-        else:
-            norms = lax.fori_loop(0, 6 * T // UNROLL, update, norms)
+        norms = lax.fori_loop(0, 6 * T // UNROLL, update, norms)
         if not last:
             norm_next = total(norms[0] + norms[1])
             ratio = norm_next / norm_now
@@ -474,7 +503,7 @@
     wall, products, jumps, lifts = exchange(
         wall_load, wall_stiff, flow_state, face_nbr, volume_ops, lift_ops, face_jac
     )
-    wall = wall.reshape(3, 2, T * 8, 128)
+    wall = wall.reshape(3 * T * 9, 128)
     vmem = pl.BlockSpec(memory_space=pltpu.VMEM)
     far = pl.BlockSpec(memory_space=pltpu.HBM)
     field = pltpu.VMEM((3 * T * 8, 128), F32)

time: 83.4 us -> 77.1 us (0.924)
  Pallas kernels: 78.6 us -> 73.8 us
  local copies, waits for them, and re-layouts: 3.67 us -> 2.17 us
    pallas_call x1, Pallas kernels: 43.5 us -> 38.6 us  [exchange(): pl.pallas_call(exchange_kernel, out_shape=(jax.ShapeDtypeStruct((3, NX, N...]
    unnamed x2, local copies, waits for them, and re-layouts: 3.67 us -> 2.17 us
where the time goes in v3:
time: 77.1 us; the launch traced here: 76.8 us
  Pallas kernels  73.8 us (96%)
  local copies, waits for them, and re-layouts  2.17 us (3%)
  between operations  0.8 us (1%)
    pallas_call x1, Pallas kernels, exchange(): pl.pallas_call(exchange_kernel, out_shape=(jax.ShapeDtypeStruct((3, NX, N...  38.6 us
    pallas_call x1, Pallas kernels, on_device(): pl.pallas_call(solve_kernel, out_shape=(jax.ShapeDtypeStruct((NQ, NE), BF...  35.2 us
    unnamed x2, local copies, waits for them, and re-layouts  2.17 us

profile of v3, /device:TPU:1, one launch (start us, length us, event | category | flops | bytes accessed | tf_op | source)
XLA Modules:
  0.0 76.8 jit_solution(3746607772344328712)
XLA Ops:
  0.6 0.9 %copy.16.jac = bf16[6,2,5,5]{3,2,1,0:T(8,128)(2,1)S(1)} copy(bf16[6,2,5,5]{0,1,3,2:T(2,128)(2,1)} %param.20) | data formatting | bytes 1200 | tf_op args[7]
  1.5 1.3 %copy.15.vol = bf16[4,270,270]{2,1,0:T(8,128)(2,1)S(1)} copy(bf16[4,270,270]{2,0,1:T(4,128)(2,1)} %param.18) | data formatting | bytes 1166400 | tf_op args[5]
  2.8 38.6 %exchange.1 = (s32[3,4,8,9,8,128]{5,4,3,2,1,0:T(8,128)S(1)}, f32[4,270,1024]{2,1,0:T(8,128)S(1)}, f32[768,1024]{1,0:T(8,128)S(1)}, bf16[270,768]{1,0:T(8,128)(2,1)S(1)}) custom-call(f32[3,8,128]{2,1,0:T(8,128)} %load.1, f32[3,8,128]{2,1,0:T(8,128)} %stiff.1, bf16[270,1024]{1,0:T(8,128)(2,1)} %flow_in.1, s32[6,1024]{1,0:T(8,128)} %nbr_in.1, ...), custom_call_target="tpu_custom_call" | custom-call | tf_op jit(solution)/shard_map/exchange/pallas_call | solution.py:309
  41.5 35.2 %solve.1 = (bf16[270,1024]{1,0:T(8,128)(2,1)}, f32[3,8,128]{2,1,0:T(8,128)}) custom-call(s32[1024]{0:T(1024)} %anchor_in.1, f32[4,1024]{1,0:T(4,128)} %base_in.1, f32[1,1024]{1,0:T(1,128)} %bitcast.3, s32[6912,128]{1,0:T(8,128)S(1)} %bitcast.2, f32[4,270,1024]{2,1,0:T(8,128)S(1)} %get-tuple-element.7.products, f32[768,1024]{1,0:T(8,128)S(1)} %get-tuple-element.8.jumps, ...), custom_call_target="tpu_custom_call" | custom-call | tf_op jit(solution)/shard_map/solve/pallas_call | solution.py:510

commit v4 on v3

--- a/solution.py
+++ b/solution.py
@@ -17,7 +17,8 @@
 ORDERS = (("z", "x", "y"), ("x", "y", "z"), ("z", "y", "x"))
 SLOTS = 24
 T = 256
-UNROLL = 64
+UNROLL = 256
+BUNROLL = 64
 STIFF_LOW, STIFF_UNIT = 0.01, 0.29 / 65535.0
 F32 = jnp.float32
 BF16 = jnp.bfloat16
@@ -182,6 +183,14 @@
     return jnp.exp2(power.astype(F32)) * (1.0 / 32767.0)
 
 
+def find_anchors(anchor, lines, columns):
+    place = anchor[...]
+    section = place >> 15
+    lines[...] = ((place >> 7) & (T - 1)) * 8 + (section & 1) * NY + (section >> 1)
+    column = lax.broadcasted_iota(jnp.int32, (128, 1), 0)
+    columns[...] = jnp.where(column == (place & 127), 1.0, 0.0)
+
+
 def volume_part(direction, flow, vol, products):
     products[direction] = dot(vol[direction], flow[...])
 
@@ -213,9 +222,9 @@
 
 
 def exchange_kernel(
-    load, stiff, flow_in, nbr_in, vol, lift_in, jac, sel_in, spread_in, same_in,
-    wall, products, jumps, lifts,
-    heads, flow, nbr, lift, sel, spread, same, cand, own_load, own_stiff,
+    load, stiff, flow_in, nbr_in, anchor_in, vol, lift_in, jac, sel_in, spread_in, same_in,
+    wall, products, jumps, lifts, lines, columns,
+    heads, flow, nbr, anchor, lift, sel, spread, same, cand, own_load, own_stiff,
     send, recv, pass_send, pass_recv, head_send, head_recv, in_sem,
 ):
     here = coordinates()
@@ -236,7 +245,7 @@
     for peer in peers:
         pl.semaphore_signal(barrier, inc=1, device_id=peer, device_id_type=MESH)
     pairs = [
-        (load, own_load), (stiff, own_stiff), (flow_in, flow), (nbr_in, nbr),
+        (load, own_load), (stiff, own_stiff), (flow_in, flow), (nbr_in, nbr), (anchor_in, anchor),
         (sel_in, sel), (spread_in, spread), (same_in, same), (lift_in, lift),
     ]
     local = [pltpu.make_async_copy(a, b, in_sem.at[i]) for i, (a, b) in enumerate(pairs)]
@@ -251,48 +260,47 @@
     pl.semaphore_wait(barrier, len(peers))
     gathers = [Gather(color, here, wall, send, recv, pass_send, pass_recv) for color in range(3)]
 
-    def advance(*events):
-        for event in events:
-            for gather in gathers:
-                gather.advance(event)
-
-    advance(0)
-    for copy in local[2:]:
-        copy.wait()
-    for direction in range(4):
-        volume_part(direction, flow, vol, products)
-    advance(1)
+    def advance(*pairs):
+        for color, event in pairs:
+            gathers[color].advance(event)
+
+    def face(number):
+        face_part(number, flow, heads, nbr, jac, sel, spread, same, jumps, cand)
+
+    advance((1, 0), (0, 0), (2, 0))
     head_copies = []
-    for face, peer in enumerate(sides):
+    for number, peer in enumerate(sides):
         copy = pltpu.make_async_remote_copy(
             src_ref=flow_in.at[:, pl.ds(0, HB)],
-            dst_ref=heads.at[face],
-            send_sem=head_send.at[face],
-            recv_sem=head_recv.at[face],
+            dst_ref=heads.at[number],
+            send_sem=head_send.at[number],
+            recv_sem=head_recv.at[number],
             device_id=peer,
             device_id_type=MESH,
         )
         copy.start()
         head_copies.append(copy)
-
-    def face(number):
-        face_part(number, flow, heads, nbr, jac, sel, spread, same, jumps, cand)
-
+    for copy in local[2:]:
+        copy.wait()
+    for direction in range(4):
+        volume_part(direction, flow, vol, products)
+    advance((1, 1), (0, 1), (2, 1))
+    find_anchors(anchor, lines, columns)
     for number in range(6):
         lifts[:, pl.ds(number * 128, NF)] = lift[number]
     face(4)
     face(5)
-    advance(2)
+    advance((1, 2), (0, 2), (2, 2))
     for copy in head_copies:
         copy.wait()
     face(0)
-    advance(3)
+    advance((1, 3), (1, 4), (0, 3), (2, 3))
     face(1)
-    advance(4)
+    advance((1, 5), (1, 6), (0, 4), (2, 4))
     face(2)
-    advance(5, 6)
+    advance((1, 7), (1, 8), (0, 5), (2, 5))
     face(3)
-    advance(7, 8, 9)
+    advance((1, 9),)
     for gather in gathers:
         gather.finish()
 
@@ -301,7 +309,7 @@
     return pltpu.with_memory_space_constraint(x, pltpu.HBM)
 
 
-def exchange(wall_load, wall_stiff, flow_state, face_nbr, volume_ops, lift_ops, face_jac):
+def exchange(wall_load, wall_stiff, flow_state, face_nbr, wall_anchor, volume_ops, lift_ops, face_jac):
     vmem = pl.BlockSpec(memory_space=pltpu.VMEM)
     far = pl.BlockSpec(memory_space=pltpu.HBM)
     spread, same = expansion()
@@ -313,13 +321,16 @@
             jax.ShapeDtypeStruct((4, NQ, NE), F32),
             jax.ShapeDtypeStruct((768, NE), F32),
             jax.ShapeDtypeStruct((NQ, 768), BF16),
+            jax.ShapeDtypeStruct((1, NE), jnp.int32),
+            jax.ShapeDtypeStruct((128, NE), F32),
         ),
-        in_specs=[far] * 4 + [vmem, far, vmem] + [far] * 3,
-        out_specs=(vmem,) * 4,
+        in_specs=[far] * 5 + [vmem, far, vmem] + [far] * 3,
+        out_specs=(vmem,) * 6,
         scratch_shapes=[
             pltpu.VMEM((4, NQ, HB), BF16),
             pltpu.VMEM((NQ, NE), BF16),
             pltpu.VMEM((6, NE), jnp.int32),
+            pltpu.VMEM((1, NE), jnp.int32),
             pltpu.VMEM((6, NQ, NF), BF16),
             pltpu.VMEM((6, 128, NQ), BF16),
             pltpu.VMEM((128, 5), BF16),
@@ -333,12 +344,12 @@
             dma((3 * 2 * NZ,)),
             dma((4,)),
             dma((4,)),
-            dma((8,)),
+            dma((9,)),
         ],
         compiler_params=pltpu.CompilerParams(collective_id=0, has_side_effects=True, vmem_limit_bytes=32 << 20),
         name="exchange",
     )(
-        *map(stay, (wall_load, wall_stiff, flow_state, face_nbr)),
+        *map(stay, (wall_load, wall_stiff, flow_state, face_nbr, wall_anchor.reshape(1, NE))),
         volume_ops,
         stay(lift_ops),
         face_jac,
@@ -358,103 +369,110 @@
     def total(acc):
         return jnp.sum(jnp.sum(acc, axis=0, keepdims=True), axis=1, keepdims=True)
 
+    def wide(value):
+        return jnp.broadcast_to(value, (8, 128))
+
     def previous(v):
         return jnp.where(sub >= 4, pltpu.roll(v, 4, 0), jnp.where(sub == 0, 0.0, pltpu.roll(v, 5, 0)))
 
     def following(v):
         return jnp.where(sub < 4, pltpu.roll(v, 4, 0), jnp.where(sub == 7, 0.0, pltpu.roll(v, 3, 0)))
 
-    ratio = norm_now = None
-    steps = []
-    for iteration in range(ITERS):
-        first, last = iteration == 0, iteration == ITERS - 1
-        old, new = searches[(iteration + 1) % 2], searches[iteration % 2]
-        if not first:
-            ratio_b = jnp.broadcast_to(ratio, (8, 128))
+    def apply(old, new, ratio, first=False, last=False):
+        units = {}
+
+        def packed(c, b, u):
+            group = (c * T + b * UNROLL) // 8 + u // 8
+            return group, wall[rows(group * 9 + u % 8), :]
 
         def direction(c, b, u):
             if not first:
                 i = rows(c * T + b * UNROLL + u)
-                return resid[i, :] + ratio_b * old[i, :]
-            group = (c * T + b * UNROLL) // 8 + u // 8
-            if (c, u // 8) not in units:
-                units[c, u // 8] = load_unit(wall[rows(group * 9 + 8), :])
-            return (wall[rows(group * 9 + u % 8), :] >> 16).astype(F32) * units[c, u // 8]
-
-        def stiffness(c, b, u):
-            group = (c * T + b * UNROLL) // 8 + u // 8
-            code = wall[rows(group * 9 + u % 8), :] & 65535
-            return (4.0 + STIFF_LOW) + code.astype(F32) * STIFF_UNIT
-
-        sums = (zero, zero)
-        norms = (zero, zero)
+                return resid[i, :] + ratio * old[i, :]
+            group, word = packed(c, b, u)
+            if u // 8 not in units:
+                units[u // 8] = load_unit(wall[rows(group * 9 + 8), :])
+            return (word >> 16).astype(F32) * units[u // 8]
+
+        sums = norms = (zero, zero)
         for c in range(3):
-            units = {}
+            units.clear()
             top = direction(c, 0, 0)
-            units = {}
+            units.clear()
             bottom = direction(c, T // UNROLL - 1, UNROLL - 1)
-
-            def one(b, u, above, here, below, sums, norms):
-                i = rows(c * T + b * UNROLL + u)
-                left = jnp.where(lane == 0, 0.0, pltpu.roll(here, 1, 1))
-                right = jnp.where(lane == 127, 0.0, pltpu.roll(here, 127, 1))
-                if first:
-                    middle = stiffness(c, b, u)
-                    diag[i, :] = middle
-                    norms = (norms[1], norms[0] + here * here)
-                else:
-                    middle = diag[i, :]
-                value = middle * here - ((above + below) + (left + right))
-                if not last:
-                    image[i, :] = value
-                new[i, :] = here
-                return (sums[1], sums[0] + here * value), norms
 
             def block(b, carry, ends=False):
                 above, here, sums, norms = carry
                 units.clear()
                 for u in range(UNROLL):
-                    if ends and u == UNROLL - 1:
-                        below = following(top)
+                    i = rows(c * T + b * UNROLL + u)
+                    below = following(top) if ends and u == UNROLL - 1 else direction(c, b, u + 1)
+                    left = jnp.where(lane == 0, 0.0, pltpu.roll(here, 1, 1))
+                    right = jnp.where(lane == 127, 0.0, pltpu.roll(here, 127, 1))
+                    if first:
+                        code = packed(c, b, u)[1] & 65535
+                        middle = (4.0 + STIFF_LOW) + code.astype(F32) * STIFF_UNIT
+                        diag[i, :] = middle
+                        norms = (norms[1], norms[0] + here * here)
                     else:
-                        below = direction(c, b, u + 1)
-                    sums, norms = one(b, u, above, here, below, sums, norms)
+                        middle = diag[i, :]
+                    value = middle * here - ((above + below) + (left + right))
+                    if not last:
+                        image[i, :] = value
+                    new[i, :] = here
+                    sums = (sums[1], sums[0] + here * value)
                     above, here = here, below
                 return above, here, sums, norms
 
             carry = (previous(bottom), top, sums, norms)
-            carry = lax.fori_loop(0, T // UNROLL - 1, block, carry)
+            if T > UNROLL:
+                carry = lax.fori_loop(0, T // UNROLL - 1, block, carry)
             _, _, sums, norms = block(T // UNROLL - 1, carry, ends=True)
-        if first:
-            norm_now = total(norms[0] + norms[1])
-        step = jnp.broadcast_to(norm_now / total(sums[0] + sums[1]), (8, 128))
-        steps.append(step)
-        def update(b, norms):
-            for u in range(UNROLL // 2):
-                i = rows(b * (UNROLL // 2) + u)
-                if iteration % 2 == 1:
-                    gain = steps[iteration - 1] * old[i, :] + step * new[i, :]
-                    disp[i, :] = gain if iteration == 1 else disp[i, :] + gain
-                if not last:
-                    held = (new if first else resid)[i, :] - step * image[i, :]
+        return total(sums[0] + sums[1]), total(norms[0] + norms[1]) if first else None
+
+    def update(step, source, moves, add=True, norm=True):
+        def block(b, norms):
+            for u in range(BUNROLL):
+                i = rows(b * BUNROLL + u)
+                if moves:
+                    gain = moves[0][0] * moves[0][1][i, :]
+                    for size, field in moves[1:]:
+                        gain = gain + size * field[i, :]
+                    disp[i, :] = disp[i, :] + gain if add else gain
+                if norm:
+                    held = source[i, :] - step * image[i, :]
                     resid[i, :] = held
                     norms = (norms[1], norms[0] + held * held)
             return norms
 
-        norms = (zero, zero)
-        norms = lax.fori_loop(0, 6 * T // UNROLL, update, norms)
-        if not last:
-            norm_next = total(norms[0] + norms[1])
-            ratio = norm_next / norm_now
-            norm_now = norm_next
+        norms = lax.fori_loop(0, 3 * T // BUNROLL, block, (zero, zero))
+        return total(norms[0] + norms[1]) if norm else None
+
+    even, odd = searches
+    product, norm = apply(None, even, None, first=True)
+    step = wide(norm / product)
+    norm_next = update(step, even, [(step, even)], add=False)
+
+    def pair(_, carry):
+        norm, norm_next = carry
+        product, _ = apply(even, odd, wide(norm_next / norm))
+        first_step = wide(norm_next / product)
+        norm, norm_next = norm_next, update(first_step, resid, [])
+        product, _ = apply(odd, even, wide(norm_next / norm))
+        step = wide(norm_next / product)
+        return norm_next, update(step, resid, [(first_step, odd), (step, even)])
+
+    norm, norm_next = lax.fori_loop(0, (ITERS - 2) // 2, pair, (norm, norm_next))
+    product, _ = apply(even, odd, wide(norm_next / norm), last=True)
+    update(None, None, [(wide(norm_next / product), odd)], norm=False)
 
 
 def solve_kernel(
-    anchor_in, base_in, weight_in, wall, products, jumps, lifts,
+    base_in, weight_in, wall, products, jumps, lifts, lines_in, columns,
     out, own_disp,
-    disp, resid, search_a, search_b, image, diag, picked, flux, anchor, base, weight, in_sem,
+    disp, resid, search_a, search_b, image, diag, picked, flux, lines, base, weight, in_sem,
 ):
-    pairs = [(anchor_in, anchor), (base_in, base), (weight_in, weight)]
+    pairs = [(lines_in, lines), (base_in, base), (weight_in, weight)]
     local = [pltpu.make_async_copy(a, b, in_sem.at[i]) for i, (a, b) in enumerate(pairs)]
     for copy in local:
         copy.start()
@@ -466,27 +484,24 @@
     for c in range(3):
         for i in range(8):
             own_disp[c, pl.ds(i, 1), :] = disp[pl.ds((c * T + dom * 8 + i) * 8 + line, 1), :]
-    lane = lax.broadcasted_iota(jnp.int32, (1, 128), 1)
 
     def pick(e, carry):
-        a = anchor[e]
-        s = a >> 15
-        at = ((a >> 7) & (T - 1)) * 8 + (s & 1) * NY + (s >> 1)
-        hit = lane == (a & 127)
+        at = lines[0, e]
         for c in range(3):
-            picked[c, pl.ds(e, 1), :] = jnp.where(hit, disp[pl.ds(c * T * 8 + at, 1), :], 0.0)
+            picked[c, pl.ds(e, 1), :] = disp[pl.ds(c * T * 8 + at, 1), :]
         return carry
 
-    lax.fori_loop(0, NE, pick, 0, unroll=16)
-    ones = jnp.ones((8, 128), F32)
+    lax.fori_loop(0, NE, pick, 0, unroll=32)
     geometry = []
     for k in range(4):
         row = base[pl.ds(k, 1), :]
         if k < 3:
-            at = lax.dot_general(
-                ones, picked[k], (((1,), (1,)), ((), ())), preferred_element_type=F32, precision=lax.Precision.HIGHEST
-            )
-            row = row * jnp.exp(weight[...] * at[:1])
+            found = []
+            for start in range(0, NE, 128):
+                turned = jnp.transpose(picked[k, pl.ds(start, 128), :])
+                chosen = jnp.where(columns[:, pl.ds(start, 128)] != 0.0, turned, 0.0)
+                found.append(jnp.sum(chosen, axis=0, keepdims=True))
+            row = row * jnp.exp(weight[...] * jnp.concatenate(found, axis=1))
         geometry.append(row)
     for face in range(6):
         at = pl.ds(face * 128, 128)
@@ -500,8 +515,8 @@
 def on_device(
     flow_state, base_geometry, anchor_weight, wall_anchor, face_nbr, volume_ops, lift_ops, face_jac, wall_load, wall_stiff
 ):
-    wall, products, jumps, lifts = exchange(
-        wall_load, wall_stiff, flow_state, face_nbr, volume_ops, lift_ops, face_jac
+    wall, *prepared = exchange(
+        wall_load, wall_stiff, flow_state, face_nbr, wall_anchor, volume_ops, lift_ops, face_jac
     )
     wall = wall.reshape(3 * T * 9, 128)
     vmem = pl.BlockSpec(memory_space=pltpu.VMEM)
@@ -513,13 +528,13 @@
             jax.ShapeDtypeStruct((NQ, NE), BF16),
             jax.ShapeDtypeStruct((3, 8, 128), F32),
         ),
-        in_specs=[far] * 3 + [vmem] * 4,
+        in_specs=[far] * 2 + [vmem] * 6,
         out_specs=(vmem, vmem),
         scratch_shapes=[field] * 6
         + [
             pltpu.VMEM((3, NE, 128), F32),
             pltpu.VMEM((768, NE), BF16),
-            pltpu.SMEM((NE,), jnp.int32),
+            pltpu.SMEM((1, NE), jnp.int32),
             pltpu.VMEM((4, NE), F32),
             pltpu.VMEM((1, NE), F32),
             pltpu.SemaphoreType.DMA((3,)),
@@ -527,7 +542,7 @@
         compiler_params=pltpu.CompilerParams(vmem_limit_bytes=28 << 20),
         name="solve",
     )(
-        *map(stay, (wall_anchor, base_geometry, anchor_weight.reshape(1, NE))), wall, products, jumps, lifts
+        *map(stay, (base_geometry, anchor_weight.reshape(1, NE))), wall, *prepared
     )
 
 

time: 77.1 us -> 65.2 us (0.85)
  Pallas kernels: 73.8 us -> 61.9 us
    pallas_call x1, Pallas kernels: 35.2 us -> 25.3 us  [on_device(): pl.pallas_call(solve_kernel, out_shape=(jax.ShapeDtypeStruct((NQ, NE), BF...]
    pallas_call x1, Pallas kernels: 38.6 us -> 36.7 us  [exchange(): pl.pallas_call(exchange_kernel, out_shape=(jax.ShapeDtypeStruct((3, NX, N...]
where the time goes in v4:
time: 65.2 us; the launch traced here: 64.9 us
  Pallas kernels  61.9 us (95%)
  local copies, waits for them, and re-layouts  2.17 us (3%)
  between operations  0.8 us (1%)
    pallas_call x1, Pallas kernels, exchange(): pl.pallas_call(exchange_kernel, out_shape=(jax.ShapeDtypeStruct((3, NX, N...  36.7 us
    pallas_call x1, Pallas kernels, on_device(): pl.pallas_call(solve_kernel, out_shape=(jax.ShapeDtypeStruct((NQ, NE), BF...  25.3 us
    unnamed x2, local copies, waits for them, and re-layouts  2.17 us

profile of v4, /device:TPU:1, one launch (start us, length us, event | category | flops | bytes accessed | tf_op | source)
XLA Modules:
  0.0 64.9 jit_solution(15609342537977587876)
XLA Ops:
  0.6 0.9 %copy.16.jac = bf16[6,2,5,5]{3,2,1,0:T(8,128)(2,1)S(1)} copy(bf16[6,2,5,5]{0,1,3,2:T(2,128)(2,1)} %param.20) | data formatting | bytes 1200 | tf_op args[7]
  1.5 1.3 %copy.15.vol = bf16[4,270,270]{2,1,0:T(8,128)(2,1)S(1)} copy(bf16[4,270,270]{2,0,1:T(4,128)(2,1)} %param.18) | data formatting | bytes 1166400 | tf_op args[5]
  2.8 36.7 %exchange.1 = (s32[3,4,8,9,8,128]{5,4,3,2,1,0:T(8,128)S(1)}, f32[4,270,1024]{2,1,0:T(8,128)S(1)}, f32[768,1024]{1,0:T(8,128)S(1)}, bf16[270,768]{1,0:T(8,128)(2,...) custom-call(f32[3,8,128]{2,1,0:T(8,128)} %load.1, f32[3,8,128]{2,1,0:T(8,128)} %stiff.1, ...), custom_call_target="tpu_custom_call" | custom-call | tf_op jit(solution)/shard_map/exchange/pallas_call | solution.py:317
  39.5 25.3 %solve.1 = (bf16[270,1024]{1,0:T(8,128)(2,1)}, f32[3,8,128]{2,1,0:T(8,128)}) custom-call(f32[4,1024]{1,0:T(4,128)} %base_in.1, f32[1,1024]{1,0:T(1,128)} %bitcast.5, s32[6912,128]{1,0:T(8,128)S(1)} %bitcast.3, f32[4,270,1024]{2,1,0:T(8,128)S(1)} %get-tuple-element.9.products, f32[768,1024]{1,0:T(8,128)S(1)} %get-tuple-element.10.jumps, ...), custom_call_target="tpu_custom_call" | custom-call | tf_op jit(solution)/shard_map/solve/pallas_call | solution.py:525

commit v5 on v4

--- a/solution.py
+++ b/solution.py
@@ -34,12 +34,14 @@
 
 
 def expansion():
-    spread = np.zeros((128, 5), np.float32)
-    spread[np.arange(NF), np.arange(NF) // 18] = 1.0
+    inside, entry = np.arange(NF), np.arange(25)
+    down = np.zeros((128, 128), np.float32)
+    down[:NF, :25] = inside[:, None] // 18 == entry[None, :] // 5
+    across = np.zeros((128, 128), np.float32)
+    across[:25, :NF] = entry[:, None] % 5 == inside[None, :] // 18
     same = np.zeros((128, 128), np.float32)
-    inside = np.arange(NF)
     same[:NF, :NF] = inside[:, None] % 18 == inside[None, :] % 18
-    return spread, same
+    return down, across, same
 
 
 def coordinates():
@@ -192,10 +194,21 @@
 
 
 def volume_part(direction, flow, vol, products):
-    products[direction] = dot(vol[direction], flow[...])
-
-
-def face_part(face, flow, heads, nbr, jac, sel, spread, same, jumps, cand):
+    products[direction] = dot(vol[:, direction, :], flow[...])
+
+
+def flux_entries(jac, table, entries):
+    table[...] = jnp.zeros_like(table)
+    for v in range(5):
+        for w in range(5):
+            both = jac[v, w].astype(F32)
+            for side in range(2):
+                table[side, pl.ds(v * 5 + w, 1), pl.ds(0, 6)] = both[side : side + 1]
+    for side in range(2):
+        entries[side] = jnp.transpose(table[side])
+
+
+def face_part(face, flow, heads, nbr, entries, sel, down, across, same, jumps, cand):
     state = flow[...]
     row = lax.broadcasted_iota(jnp.int32, (256, 1), 0).astype(F32).astype(BF16)
     other = sel[face ^ 1]
@@ -215,16 +228,16 @@
     mine = dot(sel[face], state)
     mixes = []
     for side in range(2):
-        wide = dot(spread[...], jac[face, side]).astype(BF16)
-        wide = lax.dot_general(wide, spread[...], (((1,), (1,)), ((), ())), preferred_element_type=F32)
+        tall = (down[...] * entries[side, pl.ds(face, 1), :]).astype(BF16)
+        wide = dot(tall, across[...])
         mixes.append((wide * same[...]).astype(BF16))
     jumps[pl.ds(face * 128, 128), :] = dot(mixes[0], mine.astype(BF16)) + dot(mixes[1], theirs.astype(BF16))
 
 
 def exchange_kernel(
-    load, stiff, flow_in, nbr_in, anchor_in, vol, lift_in, jac, sel_in, spread_in, same_in,
+    load, stiff, flow_in, nbr_in, anchor_in, vol_in, lift_in, jac_in, sel_in, down_in, across_in, same_in,
     wall, products, jumps, lifts, lines, columns,
-    heads, flow, nbr, anchor, lift, sel, spread, same, cand, own_load, own_stiff,
+    heads, flow, nbr, anchor, vol, lift, jac, sel, down, across, same, table, entries, cand, own_load, own_stiff,
     send, recv, pass_send, pass_recv, head_send, head_recv, in_sem,
 ):
     here = coordinates()
@@ -246,7 +259,8 @@
         pl.semaphore_signal(barrier, inc=1, device_id=peer, device_id_type=MESH)
     pairs = [
         (load, own_load), (stiff, own_stiff), (flow_in, flow), (nbr_in, nbr), (anchor_in, anchor),
-        (sel_in, sel), (spread_in, spread), (same_in, same), (lift_in, lift),
+        (vol_in, vol), (jac_in, jac),
+        (sel_in, sel), (down_in, down), (across_in, across), (same_in, same), (lift_in, lift),
     ]
     local = [pltpu.make_async_copy(a, b, in_sem.at[i]) for i, (a, b) in enumerate(pairs)]
     for copy in local:
@@ -265,7 +279,7 @@
             gathers[color].advance(event)
 
     def face(number):
-        face_part(number, flow, heads, nbr, jac, sel, spread, same, jumps, cand)
+        face_part(number, flow, heads, nbr, entries, sel, down, across, same, jumps, cand)
 
     advance((1, 0), (0, 0), (2, 0))
     head_copies = []
@@ -282,9 +296,12 @@
         head_copies.append(copy)
     for copy in local[2:]:
         copy.wait()
-    for direction in range(4):
+    for direction in range(2):
         volume_part(direction, flow, vol, products)
     advance((1, 1), (0, 1), (2, 1))
+    for direction in range(2, 4):
+        volume_part(direction, flow, vol, products)
+    flux_entries(jac, table, entries)
     find_anchors(anchor, lines, columns)
     for number in range(6):
         lifts[:, pl.ds(number * 128, NF)] = lift[number]
@@ -312,7 +329,7 @@
 def exchange(wall_load, wall_stiff, flow_state, face_nbr, wall_anchor, volume_ops, lift_ops, face_jac):
     vmem = pl.BlockSpec(memory_space=pltpu.VMEM)
     far = pl.BlockSpec(memory_space=pltpu.HBM)
-    spread, same = expansion()
+    down, across, same = expansion()
     dma = pltpu.SemaphoreType.DMA
     return pl.pallas_call(
         exchange_kernel,
@@ -324,17 +341,22 @@
             jax.ShapeDtypeStruct((1, NE), jnp.int32),
             jax.ShapeDtypeStruct((128, NE), F32),
         ),
-        in_specs=[far] * 5 + [vmem, far, vmem] + [far] * 3,
+        in_specs=[far] * 12,
         out_specs=(vmem,) * 6,
         scratch_shapes=[
             pltpu.VMEM((4, NQ, HB), BF16),
             pltpu.VMEM((NQ, NE), BF16),
             pltpu.VMEM((6, NE), jnp.int32),
             pltpu.VMEM((1, NE), jnp.int32),
+            pltpu.VMEM((NQ, 4, NQ), BF16),
             pltpu.VMEM((6, NQ, NF), BF16),
+            pltpu.VMEM((5, 5, 2, 6), BF16),
             pltpu.VMEM((6, 128, NQ), BF16),
-            pltpu.VMEM((128, 5), BF16),
             pltpu.VMEM((128, 128), F32),
+            pltpu.VMEM((128, 128), BF16),
+            pltpu.VMEM((128, 128), F32),
+            pltpu.VMEM((2, 128, 128), F32),
+            pltpu.VMEM((2, 128, 128), F32),
             pltpu.VMEM((128, NE + HB), BF16),
             pltpu.VMEM((3, 8, 128), F32),
             pltpu.VMEM((3, 8, 128), F32),
@@ -344,16 +366,20 @@
             dma((3 * 2 * NZ,)),
             dma((4,)),
             dma((4,)),
-            dma((9,)),
+            dma((12,)),
         ],
         compiler_params=pltpu.CompilerParams(collective_id=0, has_side_effects=True, vmem_limit_bytes=32 << 20),
         name="exchange",
     )(
-        *map(stay, (wall_load, wall_stiff, flow_state, face_nbr, wall_anchor.reshape(1, NE))),
-        volume_ops,
-        stay(lift_ops),
-        face_jac,
-        *map(stay, (jnp.asarray(selection(), BF16), jnp.asarray(spread, BF16), jnp.asarray(same, F32))),
+        *map(
+            stay,
+            (
+                wall_load, wall_stiff, flow_state, face_nbr, wall_anchor.reshape(1, NE),
+                jnp.transpose(volume_ops, (1, 0, 2)), lift_ops, jnp.transpose(face_jac, (2, 3, 1, 0)),
+                jnp.asarray(selection(), BF16), jnp.asarray(down, F32), jnp.asarray(across, BF16),
+                jnp.asarray(same, F32),
+            ),
+        )
     )
 
 

time: 65.2 us -> 62.8 us (0.963)
  local copies, waits for them, and re-layouts: 2.17 us -> 0 us
    unnamed x2 -> x0, local copies, waits for them, and re-layouts: 2.17 us -> none
where the time goes in v5:
time: 62.8 us; the launch traced here: 62.6 us
  Pallas kernels  61.8 us (98%)
  between operations  0.8 us (1%)
    pallas_call x1, Pallas kernels, exchange(): pl.pallas_call(exchange_kernel, out_shape=(jax.ShapeDtypeStruct((3, NX, N...  36.6 us
    pallas_call x1, Pallas kernels, on_device(): pl.pallas_call(solve_kernel, out_shape=(jax.ShapeDtypeStruct((NQ, NE), BF...  25.2 us

profile of v5, /device:TPU:1, one launch (start us, length us, event | category | flops | bytes accessed | tf_op | source)
XLA Modules:
  0.0 62.6 jit_solution(17201501541375780604)
XLA Ops:
  0.6 36.6 %exchange.1 = (s32[3,4,8,9,8,128]{5,4,3,2,1,0:T(8,128)S(1)}, f32[4,270,1024]{2,1,0:T(8,128)S(1)}, f32[768,1024]{1,0:T(8,128)S(1)}, bf16[270,768]{1,0:T(8,128)(2,...) custom-call(f32[3,8,128]{2,1,0:T(8,128)} %load.1, f32[3,8,128]{2,1,0:T(8,128)} %stiff.1, ...), custom_call_target="tpu_custom_call" | custom-call | tf_op jit(solution)/shard_map/exchange/pallas_call | solution.py:334
  37.2 25.2 %solve.1 = (bf16[270,1024]{1,0:T(8,128)(2,1)}, f32[3,8,128]{2,1,0:T(8,128)}) custom-call(f32[4,1024]{1,0:T(4,128)} %base_in.1, f32[1,1024]{1,0:T(1,128)} %bitcast.9, s32[6912,128]{1,0:T(8,128)S(1)} %bitcast.5, f32[4,270,1024]{2,1,0:T(8,128)S(1)} %get-tuple-element.9.products, f32[768,1024]{1,0:T(8,128)S(1)} %get-tuple-element.10.jumps, ...), custom_call_target="tpu_custom_call" | custom-call | tf_op jit(solution)/shard_map/solve/pallas_call | solution.py:551

commit v6 on v5

--- a/solution.py
+++ b/solution.py
@@ -502,9 +502,9 @@
     local = [pltpu.make_async_copy(a, b, in_sem.at[i]) for i, (a, b) in enumerate(pairs)]
     for copy in local:
         copy.start()
+    solve_wall(wall, disp, resid, (search_a, search_b), image, diag)
     for copy in local:
         copy.wait()
-    solve_wall(wall, disp, resid, (search_a, search_b), image, diag)
     sec, dom = lax.axis_index("sec"), lax.axis_index("dom")
     line = (sec % NC) * NY + sec // NC
     for c in range(3):

time: 62.8 us -> 62 us (0.987)
  Pallas kernels: 61.8 us -> 61 us
    pallas_call x1, Pallas kernels: 25.2 us -> 24.5 us  [on_device(): pl.pallas_call(solve_kernel, out_shape=(jax.ShapeDtypeStruct((NQ, NE), BF...]
where the time goes in v6:
time: 62 us; the launch traced here: 61.9 us
  Pallas kernels  61 us (98%)
  between operations  0.8 us (1%)
    pallas_call x1, Pallas kernels, exchange(): pl.pallas_call(exchange_kernel, out_shape=(jax.ShapeDtypeStruct((3, NX, N...  36.6 us
    pallas_call x1, Pallas kernels, on_device(): pl.pallas_call(solve_kernel, out_shape=(jax.ShapeDtypeStruct((NQ, NE), BF...  24.5 us

profile of v6, /device:TPU:1, one launch (start us, length us, event | category | flops | bytes accessed | tf_op | source)
XLA Modules:
  0.0 61.9 jit_solution(15706080172967661698)
XLA Ops:
  0.6 36.6 %exchange.1 = (s32[3,4,8,9,8,128]{5,4,3,2,1,0:T(8,128)S(1)}, f32[4,270,1024]{2,1,0:T(8,128)S(1)}, f32[768,1024]{1,0:T(8,128)S(1)}, bf16[270,768]{1,0:T(8,128)(2,...) custom-call(f32[3,8,128]{2,1,0:T(8,128)} %load.1, f32[3,8,128]{2,1,0:T(8,128)} %stiff.1, ...), custom_call_target="tpu_custom_call" | custom-call | tf_op jit(solution)/shard_map/exchange/pallas_call | solution.py:334
  37.2 24.5 %solve.1 = (bf16[270,1024]{1,0:T(8,128)(2,1)}, f32[3,8,128]{2,1,0:T(8,128)}) custom-call(f32[4,1024]{1,0:T(4,128)} %base_in.1, f32[1,1024]{1,0:T(1,128)} %bitcast.9, s32[6912,128]{1,0:T(8,128)S(1)} %bitcast.5, f32[4,270,1024]{2,1,0:T(8,128)S(1)} %get-tuple-element.9.products, f32[768,1024]{1,0:T(8,128)S(1)} %get-tuple-element.10.jumps, ...), custom_call_target="tpu_custom_call" | custom-call | tf_op jit(solution)/shard_map/solve/pallas_call | solution.py:551
